TPU v7x, 32 devices: a whole 2x2x4 slice. The times are simulated.
32 devices in a mesh: tiles: 16 (over z, y, x), grp: 2 (over core).
Axes of the slice: x: 2, y: 2, z: 4, core: 2. Of those that a mesh axis runs over, the one named last changes fastest.
Arguments:
- strips: bfloat16 [64, 256, 4096], P(('tiles', 'grp'))
- edge_colour: int32 [32, 2], P(('tiles', 'grp')), may hold values from 0 to 1, as said below
- patch_offsets: int32 [32, 2, 16, 2], P(('tiles', 'grp')), may hold values from 0 to 3968, as said below
- patch_live: int32 [32, 2], P(('tiles', 'grp')), may hold values from 4 to 16
- node_ids: int32 [32, 2, 16], P(('tiles', 'grp')), may hold values from 0 to 4095
Outputs:
- node_sums: float32 [2, 4096], P(None, ('tiles', 'grp'))
Inputs may be any that keep to these rules, and one draw needn't show every extreme that they name: `edge_colour`: for each device its 2 entries name different strips. `patch_offsets`: A device and the device it is paired with in a round have the same offsets in that round. Rows are at most 128.
All inputs are finite; a program needn't handle non-finite values.
Results may differ from a plain program's by a relative error of at most 0.0003.
Values may be sent and summed in bfloat16 or wider, within the bound.
A program may use at most 64 MiB of HBM per device.

v0:
```python
import functools
import math

import jax
import jax.numpy as jnp
import numpy as np
from jax import lax
from jax.experimental import pallas as pl
from jax.experimental.pallas import tpu as pltpu
from jax.sharding import PartitionSpec as P

PATCH = 128
NODE_DEV = 128
LANES = 128
PACK = 4
GROUP = 4

F32 = jnp.float32
BF16 = jnp.bfloat16
VMEM = pltpu.MemorySpace.VMEM
SMEM = pltpu.MemorySpace.SMEM


def split_np(x):
    hi = np.asarray(x, np.float32).astype(BF16)
    lo = (np.asarray(x, np.float64) - hi.astype(np.float64)).astype(np.float32).astype(BF16)
    return hi, lo


def tables():
    n = PATCH
    j = np.arange(n)
    angle = 2.0 * math.pi / n * ((j[:, None] * j[None, :]) % n)
    c, s = np.cos(angle), np.sin(angle)
    chi, clo = split_np(np.concatenate([c, s], axis=1))
    col = np.concatenate([chi, clo], axis=0)
    rhi, rlo = split_np(np.block([[c, -s], [s, c]]))
    row = np.concatenate([rhi, rlo, rhi], axis=1)
    ihi, ilo = split_np(np.concatenate([c, s], axis=1))
    inv_row = np.concatenate([ihi, ilo, ihi], axis=1)
    weight = np.where((j == 0) | (j == n // 2), 1.0, 2.0)[:, None]
    packed = np.where(j[:, None] <= n // 2, weight * c, -2.0 * s) / float(n * n)
    vhi, vlo = split_np(packed)
    inv_col = np.concatenate([vhi, vlo, vhi], axis=0)
    return col, row, inv_row, inv_col


def split(x):
    hi = x.astype(BF16)
    return hi, (x - hi.astype(F32)).astype(BF16)


def dot(a, b):
    return jnp.dot(a, b, preferred_element_type=F32)


def extract(half, colour_ref, offset_ref, live_ref, ids_ref, strip_ref, kept_ref, sent_ref, line_ref, tmp_ref):
    n = PATCH
    slots = 2 * half
    rnd = pl.program_id(0)
    tile = lax.axis_index("tiles")
    side = jnp.where(rnd == 0, tile % 2, (tile // (lax.axis_size("tiles") // 2)) % 2)
    height, width = strip_ref.shape[1], strip_ref.shape[2]
    rows = []
    for j in range(slots):
        k = (side * half + half + j) % slots
        row, column = offset_ref[0, rnd, 0, k], offset_ref[0, rnd, 1, k]
        left = jnp.minimum(lax.div(column, LANES), width // LANES - 2) * LANES
        upper = jnp.minimum(lax.div(row, 16), (height - n) // 16 - 1) * 16
        block = strip_ref[
            0, pl.ds(pl.multiple_of(upper, 16), n + 16), pl.ds(pl.multiple_of(left, LANES), 2 * LANES)
        ].astype(F32)
        shift = lax.rem(2 * LANES - (column - left), 2 * LANES)
        tmp_ref[j] = pltpu.roll(block, shift, 1)[:, :n]
        rows.append(row - upper)
    for j in range(slots):
        window = tmp_ref[j, pl.ds(rows[j], n), :].astype(BF16)
        ref = sent_ref if j < half else kept_ref
        ref[j % half // GROUP, j % GROUP] = window
    lane = lax.broadcasted_iota(jnp.int32, (1, LANES), 1)
    ids = jnp.zeros((1, LANES), jnp.int32)
    for r in range(live_ref.shape[1]):
        for k in range(slots):
            node = jnp.where(k < live_ref[0, r], ids_ref[0, r, k], -1)
            ids = jnp.where(lane == r * slots + k, node, ids)
    line_ref[...] = ids.astype(F32)


def row_place(column, base):
    count = column.shape[0]
    lane = lax.broadcasted_iota(jnp.int32, (count, LANES), 1)
    sub = lax.broadcasted_iota(jnp.int32, (count, LANES), 0)
    return jnp.sum(jnp.where(lane == sub + base, column, 0.0), axis=0, keepdims=True)


def spectra(windows, col, row):
    n = PATCH
    x = jnp.concatenate(windows, axis=0)
    hi, lo = split(dot(jnp.concatenate([x, x], axis=1), col))

    def stack(v):
        return jnp.concatenate(
            [
                jnp.concatenate([v[:n, :n], v[n:, :n]], axis=1),
                jnp.concatenate([v[:n, n:], v[n:, n:]], axis=1),
            ],
            axis=0,
        )

    hi, lo = stack(hi), stack(lo)
    f = dot(row, jnp.concatenate([hi, hi, lo], axis=0))
    return [(f[:n, :n], f[n:, :n]), (f[:n, n:], f[n:, n:])]


def correlate(first, second, inv_row, inv_col):
    n = PATCH
    count = len(first)
    lane = lax.broadcasted_iota(jnp.int32, (n, n), 1)
    low = lane <= n // 2
    crosses = []
    mag_sums = []
    for (r1, i1), (r2, i2) in zip(first, second):
        cross_r = r1 * r2 + i1 * i2
        cross_i = r1 * i2 - i1 * r2
        mag = jnp.sqrt(cross_r * cross_r + cross_i * cross_i)
        crosses.append((cross_r, cross_i, mag))
        mag_sums.append(jnp.sum(mag, axis=0, keepdims=True))
    mean = jnp.sum(jnp.concatenate(mag_sums, axis=0), axis=1, keepdims=True) / float(n * n)
    extra = 0.1 * mean + 1e-06
    surfaces = []
    packed = []
    sums = []
    for p in range(count):
        cross_r, cross_i, mag = crosses[p]
        inverse = 1.0 / (mag + extra[p : p + 1])
        g_r = cross_r * inverse
        g_i = cross_i * inverse
        packed.append(
            split(jnp.concatenate([jnp.where(low, g_r, g_i), jnp.where(low, -g_i, g_r)], axis=0))
        )
    surfaces_wide = []
    for p in range(0, count, 2):
        hi = jnp.concatenate([packed[p][0], packed[p + 1][0]], axis=1)
        lo = jnp.concatenate([packed[p][1], packed[p + 1][1]], axis=1)
        b = dot(inv_row, jnp.concatenate([hi, hi, lo], axis=0))
        bhi, blo = split(jnp.concatenate([b[:, :n], b[:, n:]], axis=0))
        wide = dot(jnp.concatenate([bhi, bhi, blo], axis=1), inv_col)
        surfaces_wide += [wide[:n], wide[n:]]
    for surface in surfaces_wide:
        surfaces.append(surface)
        sums.append(jnp.sum(surface, axis=0, keepdims=True))
    centre = jnp.sum(jnp.concatenate(sums, axis=0), axis=1, keepdims=True) / float(n * n)
    squares = []
    tops = []
    for p in range(count):
        deviation = surfaces[p] - centre[p : p + 1]
        squares.append(jnp.sum(deviation * deviation, axis=0, keepdims=True))
        tops.append(jnp.max(surfaces[p], axis=0, keepdims=True))
    variance = jnp.sum(jnp.concatenate(squares, axis=0), axis=1, keepdims=True) / float(n * n)
    top = jnp.max(jnp.concatenate(tops, axis=0), axis=1, keepdims=True)
    scale = 2.0 / jnp.sqrt(variance + 1e-06)
    sub = lax.broadcasted_iota(jnp.int32, (n, n), 0)
    sub_coord = ((sub + n // 2) % n - n // 2).astype(F32)
    columns = []
    rows = []
    edges = []
    for p in range(count):
        e = jnp.exp((surfaces[p] - top[p : p + 1]) * scale[p : p + 1])
        columns.append(jnp.sum(e, axis=0, keepdims=True))
        rows.append(jnp.sum(e * sub_coord, axis=0, keepdims=True))
        edges.append(e[n // 2 : n // 2 + 1, :])
    columns = jnp.concatenate(columns, axis=0)
    rows = jnp.concatenate(rows, axis=0)
    edges = jnp.concatenate(edges, axis=0)
    lane = lax.broadcasted_iota(jnp.int32, (count, n), 1)
    lane_coord = ((lane + n // 2) % n - n // 2).astype(F32)

    def total(v):
        return jnp.sum(v, axis=1, keepdims=True)

    unit = float(n // 8)
    norm = 1.0 / total(columns)
    row_shift = total(rows) * norm / unit
    col_shift = total(columns * lane_coord) * norm / unit
    row_edge = total(edges) * norm * (float(n) / unit)
    col_edge = total(jnp.where(lane == n // 2, columns, 0.0)) * norm * (float(n) / unit)
    return row_shift, col_shift, -row_shift - row_edge, -col_shift - col_edge


MESH = pl.DeviceIdType.MESH


def stitch(
    half,
    rounds,
    kept_ref,
    sent,
    line,
    col_ref,
    row_ref,
    inv_row_ref,
    inv_col_ref,
    out_ref,
    kept,
    firsts,
    arrived,
    lines,
    tile_out,
    tiles,
    kept_sem,
    window_send,
    window_recv,
    line_send,
    line_recv,
    tile_send,
    tile_recv,
    hello,
):
    n = PATCH
    slots = 2 * half
    parts = half // GROUP
    groups = lax.axis_size("grp")
    tile_count = lax.axis_size("tiles")
    devices = tile_count * groups
    tile_index = lax.axis_index("tiles")
    me = tile_index * groups + lax.axis_index("grp")
    strides = [1] + [tile_count // 2] * (rounds - 1)
    sides = [(tile_index // s) % 2 for s in strides]
    partners = [tile_index + s * (1 - 2 * side) for s, side in zip(strides, sides)]

    load = pltpu.make_async_copy(kept_ref, kept, kept_sem)
    load.start()
    barrier = pltpu.get_barrier_semaphore()

    def device(d):
        return (d // groups, d % groups)

    neighbours = []
    stride = 1
    while stride < tile_count:
        bit = (tile_index // stride) % 2
        neighbours.append((tile_index + stride * (1 - 2 * bit), lax.axis_index("grp")))
        stride *= 2
    stride = 1
    while stride < groups:
        bit = (lax.axis_index("grp") // stride) % 2
        neighbours.append((tile_index, lax.axis_index("grp") + stride * (1 - 2 * bit)))
        stride *= 2
    stages = len(neighbours)
    for at in neighbours:
        pl.semaphore_signal(barrier, inc=1, device_id=at, device_id_type=MESH)

    def neighbour(stage):
        tile, group = neighbours[0]
        for i in range(1, stages):
            tile = jnp.where(stage == i, neighbours[i][0], tile)
            group = jnp.where(stage == i, neighbours[i][1], group)
        return tile, group

    def hail(stage):
        pl.semaphore_signal(
            hello.at[stage], inc=1, device_id=neighbour(stage), device_id_type=MESH
        )

    load.wait()

    def prepare(g, carry):
        for p in range(0, GROUP, 2):
            pair = spectra([kept[g, p], kept[g, p + 1]], col_ref[...], row_ref[...])
            for q in range(2):
                for c in range(2):
                    firsts[g, p + q, c] = pair[q][c]
        return carry

    lax.fori_loop(0, 1, prepare, 0)
    pl.semaphore_wait(barrier, stages)

    def window_copy(r, part):
        g = r * parts + part
        return pltpu.make_async_remote_copy(
            src_ref=sent.at[g],
            dst_ref=arrived.at[g],
            send_sem=window_send.at[g],
            recv_sem=window_recv.at[g],
            device_id=(partners[r], lax.axis_index("grp")),
            device_id_type=MESH,
        )

    def line_copy(r):
        return pltpu.make_async_remote_copy(
            src_ref=line,
            dst_ref=lines.at[r],
            send_sem=line_send.at[r],
            recv_sem=line_recv.at[r],
            device_id=(partners[r], lax.axis_index("grp")),
            device_id_type=MESH,
        )

    for part in range(parts):
        for r in range(rounds):
            window_copy(r, part).start()
    for r in range(rounds):
        line_copy(r).start()

    early = stages - rounds * parts
    for i in range(early):
        hail(i)
        if i == early - 1:
            lax.fori_loop(1, rounds * parts, prepare, 0)
        pl.semaphore_wait(hello.at[i], 1)

    def work(g, carry):
        r = g // parts
        hail(early + g)
        pltpu.make_async_remote_copy(
            src_ref=sent.at[g],
            dst_ref=arrived.at[g],
            send_sem=window_send.at[g],
            recv_sem=window_recv.at[g],
            device_id=(partners[0], lax.axis_index("grp")),
            device_id_type=MESH,
        ).wait_recv()
        side = sides[0]
        for i in range(1, rounds):
            side = jnp.where(r == i, sides[i], side)
        seconds = []
        for p in range(0, GROUP, 2):
            seconds += spectra([arrived[g, p], arrived[g, p + 1]], col_ref[...], row_ref[...])
        a, b, c, d = correlate(
            [(firsts[g, p, 0], firsts[g, p, 1]) for p in range(GROUP)],
            seconds,
            inv_row_ref[...],
            inv_col_ref[...],
        )
        base = r * slots + (g % parts) * GROUP
        own = base + side * half
        other = base + (1 - side) * half
        row_line, col_line = carry
        pl.semaphore_wait(hello.at[early + g], 1)
        return (
            row_line + row_place(a, own) + row_place(c, other),
            col_line + row_place(b, own) + row_place(d, other),
        )

    zero = jnp.zeros((1, LANES), F32)
    row_line, col_line = lax.fori_loop(0, rounds * parts, work, (zero, zero))

    lane = lax.broadcasted_iota(jnp.int32, (1, LANES), 1)
    ids = line[...]
    id_line = zero
    for r in range(rounds):
        line_copy(r).wait()
        theirs = pltpu.roll(lines[r], jnp.where(sides[r] == 0, half, LANES - half), 1)
        in_round = (lane >= r * slots) & (lane < (r + 1) * slots)
        mine = (lane // half) % 2 == sides[r]
        id_line = id_line + jnp.where(in_round, jnp.where(mine, ids, theirs), 0.0)
    tile = jnp.concatenate([row_line, col_line, id_line, zero], axis=0)
    tile = pltpu.roll(tile, (me % PACK) * (LANES // PACK), 1)
    tile_out[...] = tile
    tiles[me] = tile

    def tile_copy(i, slot):
        return pltpu.make_async_remote_copy(
            src_ref=tile_out,
            dst_ref=tiles.at[slot],
            send_sem=tile_send.at[i],
            recv_sem=tile_recv.at[slot],
            device_id=device((me + i) % devices),
            device_id_type=MESH,
        )

    def start(i, carry):
        tile_copy(i, me).start()
        return carry

    def receive(i, carry):
        tile_copy(i, (me + i) % devices).wait_recv()
        return carry

    def drain(i, carry):
        tile_copy(i, me).wait_send()
        return carry

    lax.fori_loop(1, devices, start, 0)
    for part in range(parts):
        for r in range(rounds):
            window_copy(r, part).wait_send()
    lax.fori_loop(1, devices, receive, 0)

    node = lax.broadcasted_iota(jnp.int32, (NODE_DEV, LANES), 0).astype(F32)
    first_node = (me * NODE_DEV).astype(F32)
    onehots = []
    values = []
    for g in range(devices // PACK):
        tile = tiles[g * PACK]
        for i in range(1, PACK):
            tile = tile + tiles[g * PACK + i]
        onehots.append(jnp.where(tile[2:3] - first_node == node, 1.0, 0.0).astype(BF16))
        hi = tile.astype(BF16).astype(F32)
        rest = tile - hi
        mid = rest.astype(BF16).astype(F32)
        values.append(jnp.concatenate([hi, mid, rest - mid, jnp.zeros_like(hi)], axis=0).astype(BF16))
    result = lax.dot_general(
        jnp.concatenate(values, axis=1),
        jnp.concatenate(onehots, axis=1),
        (((1,), (1,)), ((), ())),
        preferred_element_type=F32,
    )
    out_ref[0:2] = result[0:2]
    out_ref[2:4] = result[4:6] + result[8:10]
    lax.fori_loop(1, devices, drain, 0)


def on_device(strips, edge_colour, patch_offsets, patch_live, node_ids):
    rounds, height, width = strips.shape
    n = PATCH
    slot_count = patch_offsets.shape[2]
    half = slot_count // 2
    parts = half // GROUP
    groups = rounds * parts
    devices = lax.axis_size("tiles") * lax.axis_size("grp")
    whole = pl.BlockSpec(memory_space=VMEM)
    anywhere = pl.BlockSpec(memory_space=pl.ANY)
    sem = pltpu.SemaphoreType.DMA
    windows = (groups, GROUP, n, n)
    window_spec = pl.BlockSpec((parts, GROUP, n, n), lambda r, *_: (r, 0, 0, 0))
    kept, sent, line = pl.pallas_call(
        functools.partial(extract, half),
        out_shape=[jax.ShapeDtypeStruct(windows, BF16)] * 2 + [jax.ShapeDtypeStruct((1, LANES), F32)],
        grid_spec=pltpu.PrefetchScalarGridSpec(
            num_scalar_prefetch=4,
            grid=(rounds,),
            in_specs=[pl.BlockSpec((1, height, width), lambda r, colour, *_: (colour[0, r], 0, 0))],
            out_specs=[window_spec, window_spec, pl.BlockSpec((1, LANES), lambda r, *_: (0, 0))],
            scratch_shapes=[pltpu.VMEM((slot_count, n + 16, n), F32)],
        ),
        name="extract",
    )(edge_colour, jnp.transpose(patch_offsets, (0, 1, 3, 2)), patch_live, node_ids, strips)
    sums = pl.pallas_call(
        functools.partial(stitch, half, rounds),
        out_shape=jax.ShapeDtypeStruct((4, NODE_DEV), F32),
        in_specs=[anywhere] * 2 + [whole] * 5,
        out_specs=whole,
        scratch_shapes=[
            pltpu.VMEM(windows, BF16),
            pltpu.VMEM((groups, GROUP, 2, n, n), F32),
            pltpu.VMEM(windows, BF16),
            pltpu.VMEM((rounds, 1, LANES), F32),
            pltpu.VMEM((4, LANES), F32),
            pltpu.VMEM((devices, 4, LANES), F32),
            sem(()),
            sem((groups,)),
            sem((groups,)),
            sem((rounds,)),
            sem((rounds,)),
            sem((devices,)),
            sem((devices,)),
            pltpu.SemaphoreType.REGULAR((devices.bit_length() - 1,)),
        ],
        compiler_params=pltpu.CompilerParams(collective_id=0, has_side_effects=True),
        name="stitch",
    )(kept, sent, line, *(jnp.asarray(t) for t in tables()))
    return sums[0:2] + sums[2:4]


def solution(mesh):
    placed = (
        P(("tiles", "grp"), None, None),
        P(("tiles", "grp"), None),
        P(("tiles", "grp"), None, None, None),
        P(("tiles", "grp"), None),
        P(("tiles", "grp"), None, None),
    )
    return jax.shard_map(
        on_device, mesh=mesh, in_specs=placed, out_specs=P(None, ("tiles", "grp")), check_vma=False
    )
```

profile of v0, /device:TPU:0, one launch (start us, length us, event | category | flops | bytes accessed | tf_op | source)
XLA Modules:
  0.0 33.7 jit_solution(16859704907427774619)
XLA Ops:
  0.0 4.2 %extract.1 = (bf16[4,4,128,128]{3,2,1,0:T(8,128)(2,1)}, bf16[4,4,128,128]{3,2,1,0:T(8,128)(2,1)}, f32[1,128]{1,0:T(1,128)}) custom-call(s32[1,2]{1,0:T(1,128)} %colour_ref.1, s32[1,2,2,16]{3,2,1,0:T(2,128)} %bitcast.1, s32[1,2]{1,0:T(1,128)} %live_ref.1, s32[1,2,16]{2,1,0:T(2,128)} %ids_ref.1, bf16[2,256,4096]{2,1,0:T(8,128)(2,1)} %strip_ref.1), custom_call_target="tpu_custom_call" | custom-call | tf_op jit(solution)/shard_map/extract/pallas_call | solution.py:427
  4.2 28.2 %stitch.1 = f32[4,128]{1,0:T(4,128)} custom-call(bf16[4,4,128,128]{3,2,1,0:T(8,128)(2,1)} %get-tuple-element.8.kept_ref, bf16[4,4,128,128]{3,2,1,0:T(8,128)(2,1)} %get-tuple-element.9.sent, f32[1,128]{1,0:T(1,128)} %get-tuple-element.10.line, bf16[256,256]{1,0:T(8,128)(2,1)} %constant.8.clone.col_ref, bf16[256,768]{1,0:T(8,128)(2,1)} %constant.9.clone.row_ref, ...), custom_call_target="tpu_custom_call" | custom-call | tf_op jit(solution)/shard_map/stitch/pallas_call | solution.py:439
  32.4 1.3 %slice_add_fusion = f32[2,128]{1,0:T(2,128)} fusion(f32[4,128]{1,0:T(4,128)} %stitch.1), kind=kLoop, calls=%fused_computation | loop fusion | flops 256 | bytes 3072 | tf_op jit(solution)/shard_map/add | solution.py:463
where the time goes:
time: 34 us; the launch traced here: 33.7 us
  Pallas kernels  32.4 us (95%)
  other arithmetic  1.32 us (4%)
    pallas_call x1, Pallas kernels, on_device(): pl.pallas_call(functools.partial(stitch, half, rounds), out_shape=jax.Sha...  28.2 us
    pallas_call x1, Pallas kernels, on_device(): pl.pallas_call(functools.partial(extract, half), out_shape=[jax.ShapeDtyp...  4.2 us
    add x1, other arithmetic, on_device(): return sums[0:2] + sums[2:4]  1.32 us

commit v1 on v0

v1 whole, which is shorter than its diff:
```python
import functools
import math

import jax
import jax.numpy as jnp
import numpy as np
from jax import lax
from jax.experimental import pallas as pl
from jax.experimental.pallas import tpu as pltpu
from jax.sharding import PartitionSpec as P

PATCH = 128
NODE_DEV = 128
LANES = 128
GROUP = 4
PAIR = 2
SUB = 16
LAST = ((0, 2), (2, 1), (3, 1))
VMEM_LIMIT = 67043328 - 16384

F32 = jnp.float32
BF16 = jnp.bfloat16
VMEM = pltpu.MemorySpace.VMEM
SMEM = pltpu.MemorySpace.SMEM


def split_np(x):
    hi = np.asarray(x, np.float32).astype(BF16)
    lo = (np.asarray(x, np.float64) - hi.astype(np.float64)).astype(np.float32).astype(BF16)
    return hi, lo


def tables():
    n = PATCH
    j = np.arange(n)
    angle = 2.0 * math.pi / n * ((j[:, None] * j[None, :]) % n)
    c, s = np.cos(angle), np.sin(angle)
    chi, clo = split_np(np.concatenate([c, s], axis=1))
    col = np.concatenate([chi, clo], axis=0)
    rhi, rlo = split_np(np.block([[c, -s], [s, c]]))
    row = np.concatenate([rhi, rlo, rhi], axis=1)
    ihi, ilo = split_np(np.concatenate([c, s], axis=1))
    inv_row = np.concatenate([ihi, ilo, ihi], axis=1)
    weight = np.where((j == 0) | (j == n // 2), 1.0, 2.0)[:, None]
    packed = np.where(j[:, None] <= n // 2, weight * c, -2.0 * s) / float(n * n)
    vhi, vlo = split_np(packed)
    inv_col = np.concatenate([vhi, vlo, vhi], axis=0)
    return col, row, inv_row, inv_col


def split(x):
    hi = x.astype(BF16)
    return hi, (x - hi.astype(F32)).astype(BF16)


def dot(a, b):
    return jnp.dot(a, b, preferred_element_type=F32)


def row_place(column, base):
    count = column.shape[0]
    lane = lax.broadcasted_iota(jnp.int32, (count, LANES), 1)
    sub = lax.broadcasted_iota(jnp.int32, (count, LANES), 0)
    return jnp.sum(jnp.where(lane == sub + base, column, 0.0), axis=0, keepdims=True)


def spectra(windows, col, row):
    n = PATCH
    if len(windows) == 1:
        x = windows[0]
        hi, lo = split(dot(jnp.concatenate([x, x], axis=1), col))
        hi, lo = (jnp.concatenate([v[:, :n], v[:, n:]], axis=0) for v in (hi, lo))
        f = dot(row, jnp.concatenate([hi, hi, lo], axis=0))
        return [(f[:n], f[n:])]
    x = jnp.concatenate(windows, axis=0)
    hi, lo = split(dot(jnp.concatenate([x, x], axis=1), col))

    def stack(v):
        return jnp.concatenate(
            [
                jnp.concatenate([v[:n, :n], v[n:, :n]], axis=1),
                jnp.concatenate([v[:n, n:], v[n:, n:]], axis=1),
            ],
            axis=0,
        )

    hi, lo = stack(hi), stack(lo)
    f = dot(row, jnp.concatenate([hi, hi, lo], axis=0))
    return [(f[:n, :n], f[n:, :n]), (f[:n, n:], f[n:, n:])]


def correlate(first, second, inv_row, inv_col):
    n = PATCH
    count = len(first)
    lane = lax.broadcasted_iota(jnp.int32, (n, n), 1)
    low = lane <= n // 2
    crosses = []
    mag_sums = []
    for (r1, i1), (r2, i2) in zip(first, second):
        cross_r = r1 * r2 + i1 * i2
        cross_i = r1 * i2 - i1 * r2
        mag = jnp.sqrt(cross_r * cross_r + cross_i * cross_i)
        crosses.append((cross_r, cross_i, mag))
        mag_sums.append(jnp.sum(mag, axis=0, keepdims=True))
    mean = jnp.sum(jnp.concatenate(mag_sums, axis=0), axis=1, keepdims=True) / float(n * n)
    extra = 0.1 * mean + 1e-06
    surfaces = []
    packed = []
    sums = []
    for p in range(count):
        cross_r, cross_i, mag = crosses[p]
        inverse = 1.0 / (mag + extra[p : p + 1])
        g_r = cross_r * inverse
        g_i = cross_i * inverse
        packed.append(
            split(jnp.concatenate([jnp.where(low, g_r, g_i), jnp.where(low, -g_i, g_r)], axis=0))
        )
    surfaces_wide = []
    for p in range(0, count, 2):
        some = packed[p : p + 2]
        hi = jnp.concatenate([v[0] for v in some], axis=1)
        lo = jnp.concatenate([v[1] for v in some], axis=1)
        b = dot(inv_row, jnp.concatenate([hi, hi, lo], axis=0))
        bhi, blo = split(jnp.concatenate([b[:, i * n : (i + 1) * n] for i in range(len(some))], axis=0))
        wide = dot(jnp.concatenate([bhi, bhi, blo], axis=1), inv_col)
        surfaces_wide += [wide[i * n : (i + 1) * n] for i in range(len(some))]
    for surface in surfaces_wide:
        surfaces.append(surface)
        sums.append(jnp.sum(surface, axis=0, keepdims=True))
    centre = jnp.sum(jnp.concatenate(sums, axis=0), axis=1, keepdims=True) / float(n * n)
    squares = []
    tops = []
    for p in range(count):
        deviation = surfaces[p] - centre[p : p + 1]
        squares.append(jnp.sum(deviation * deviation, axis=0, keepdims=True))
        tops.append(jnp.max(surfaces[p], axis=0, keepdims=True))
    variance = jnp.sum(jnp.concatenate(squares, axis=0), axis=1, keepdims=True) / float(n * n)
    top = jnp.max(jnp.concatenate(tops, axis=0), axis=1, keepdims=True)
    scale = 2.0 / jnp.sqrt(variance + 1e-06)
    sub = lax.broadcasted_iota(jnp.int32, (n, n), 0)
    sub_coord = ((sub + n // 2) % n - n // 2).astype(F32)
    columns = []
    rows = []
    edges = []
    for p in range(count):
        e = jnp.exp((surfaces[p] - top[p : p + 1]) * scale[p : p + 1])
        columns.append(jnp.sum(e, axis=0, keepdims=True))
        rows.append(jnp.sum(e * sub_coord, axis=0, keepdims=True))
        edges.append(e[n // 2 : n // 2 + 1, :])
    columns = jnp.concatenate(columns, axis=0)
    rows = jnp.concatenate(rows, axis=0)
    edges = jnp.concatenate(edges, axis=0)
    lane = lax.broadcasted_iota(jnp.int32, (count, n), 1)
    lane_coord = ((lane + n // 2) % n - n // 2).astype(F32)

    def total(v):
        return jnp.sum(v, axis=1, keepdims=True)

    unit = float(n // 8)
    norm = 1.0 / total(columns)
    row_shift = total(rows) * norm / unit
    col_shift = total(columns * lane_coord) * norm / unit
    row_edge = total(edges) * norm * (float(n) / unit)
    col_edge = total(jnp.where(lane == n // 2, columns, 0.0)) * norm * (float(n) / unit)
    return row_shift, col_shift, -row_shift - row_edge, -col_shift - col_edge


MESH = pl.DeviceIdType.MESH


def stitch(
    colour_ref,
    offset_ref,
    live_ref,
    ids_ref,
    strips_hbm,
    col_hbm,
    row_hbm,
    inv_row_hbm,
    inv_col_hbm,
    out_ref,
    strips,
    col_ref,
    row_ref,
    inv_row_ref,
    inv_col_ref,
    shifted,
    sent,
    firsts,
    arrived,
    line,
    lines,
    tile_out,
    tiles,
    strip_sem,
    table_sem,
    window_send,
    window_recv,
    line_send,
    line_recv,
    tile_send,
    tile_recv,
    hello,
):
    n = PATCH
    rounds, blocks, layers = strips.shape[:3]
    slots = offset_ref.shape[3]
    half = slots // 2
    entries = rounds * slots
    groups = lax.axis_size("grp")
    tile_count = lax.axis_size("tiles")
    devices = tile_count * groups
    tile_index = lax.axis_index("tiles")
    group_index = lax.axis_index("grp")
    me = tile_index * groups + group_index
    strides = [1] + [tile_count // 2] * (rounds - 1)
    sides = [(tile_index // s) % 2 for s in strides]
    partners = [tile_index + s * (1 - 2 * side) for s, side in zip(strides, sides)]

    barrier = pltpu.get_barrier_semaphore()
    neighbours = []
    stride = 1
    while stride < tile_count:
        bit = (tile_index // stride) % 2
        neighbours.append((tile_index + stride * (1 - 2 * bit), group_index))
        stride *= 2
    stride = 1
    while stride < groups:
        bit = (group_index // stride) % 2
        neighbours.append((tile_index, group_index + stride * (1 - 2 * bit)))
        stride *= 2
    stages = len(neighbours)
    for at in neighbours:
        pl.semaphore_signal(barrier, inc=1, device_id=at, device_id_type=MESH)

    strip_loads = [
        pltpu.make_async_copy(strips_hbm.at[:, :, :, pl.ds(i * LANES, LANES)], strips.at[:, i], strip_sem)
        for i in range(blocks)
    ]
    for load in strip_loads:
        load.start()
    table_loads = [
        pltpu.make_async_copy(a, b, table_sem.at[i])
        for i, (a, b) in enumerate(
            [(col_hbm, col_ref), (row_hbm, row_ref), (inv_row_hbm, inv_row_ref), (inv_col_hbm, inv_col_ref)]
        )
    ]
    for load in table_loads:
        load.start()
    pltpu.make_async_copy(strips, strips, strip_sem).wait()

    def extract(r, picks):
        rests = []
        lane = lax.broadcasted_iota(jnp.int32, (n + SUB, LANES), 1)
        for i, k in enumerate(picks):
            row, column = offset_ref[0, r, 0, k], offset_ref[0, r, 1, k]
            block = jnp.minimum(lax.div(column, LANES), blocks - 2)
            layer = jnp.minimum(lax.div(row, SUB), layers - n // SUB - 1)
            shift = column - block * LANES
            turn = lax.rem(2 * LANES - shift, LANES)
            left, right = (
                pltpu.roll(
                    strips[colour_ref[0, r], block + side, pl.ds(layer, n // SUB + 1)]
                    .reshape(n + SUB, LANES)
                    .astype(F32),
                    turn,
                    1,
                )
                for side in range(2)
            )
            shifted[i] = jnp.where(lane < LANES - shift, left, right)
            rests.append(row - layer * SUB)
        return [shifted[i, pl.ds(rest, n), :].astype(BF16) for i, rest in enumerate(rests)]

    def window_copy(r, j):
        return pltpu.make_async_remote_copy(
            src_ref=sent.at[r, j],
            dst_ref=arrived.at[r, j],
            send_sem=window_send.at[r, j],
            recv_sem=window_recv.at[r, j],
            device_id=(partners[r], group_index),
            device_id_type=MESH,
        )

    def line_copy(r):
        return pltpu.make_async_remote_copy(
            src_ref=line,
            dst_ref=lines.at[r],
            send_sem=line_send.at[r],
            recv_sem=line_recv.at[r],
            device_id=(partners[r], group_index),
            device_id_type=MESH,
        )

    def produce(r, j):
        base = (1 - sides[r]) * half
        for i, window in enumerate(extract(r, [base + j + i for i in range(PAIR)])):
            sent[r, j + i] = window

    order = list(range(rounds))[::-1]
    produce(order[0], 0)
    pl.semaphore_wait(barrier, stages)
    for r in order:
        if r != order[0]:
            produce(r, 0)
            for i in range(PAIR):
                window_copy(r + 1, half - PAIR + i).start()

        def step(p, carry, r=r):
            produce(r, p * PAIR)
            for i in range(PAIR):
                window_copy(r, (p - 1) * PAIR + i).start()
            return carry

        lax.fori_loop(1, half // PAIR, step, 0)

    lane = lax.broadcasted_iota(jnp.int32, (1, LANES), 1)
    ids = jnp.zeros((1, LANES), jnp.int32)
    for r in range(rounds):
        for k in range(slots):
            node = jnp.where(k < live_ref[0, r], ids_ref[0, r, k], -1)
            ids = jnp.where(lane == r * slots + k, node, ids)
    line[...] = ids.astype(F32)
    for i in range(PAIR):
        window_copy(0, half - PAIR + i).start()
    for load in table_loads:
        load.wait()

    def prepare(r):
        def step(p, carry):
            j = p * PAIR
            windows = extract(r, [sides[r] * half + j + i for i in range(PAIR)])
            for q in range(0, PAIR, 2):
                pair = spectra(windows[q : q + 2], col_ref[...], row_ref[...])
                for i in range(2):
                    for c in range(2):
                        firsts[r, j + q + i, c] = pair[i][c]
            return carry

        return step

    lax.fori_loop(0, 1, prepare(0), 0)
    for r in range(rounds):
        line_copy(r).start()
    lax.fori_loop(1, half // PAIR, prepare(0), 0)
    for r in range(1, rounds):
        lax.fori_loop(0, half // PAIR, prepare(r), 0)

    def hail(stage):
        pl.semaphore_signal(hello.at[stage], inc=1, device_id=neighbours[stage], device_id_type=MESH)

    def greet(stage):
        if stage > 0:
            pl.semaphore_wait(hello.at[stage - 1], 1)
        if stage < stages:
            hail(stage)

    def work(r, j, count, carry):
        for i in range(count):
            pltpu.make_async_remote_copy(
                src_ref=sent.at[r, j + i],
                dst_ref=arrived.at[r, j + i],
                send_sem=window_send.at[r, j + i],
                recv_sem=window_recv.at[r, j + i],
                device_id=(partners[r], group_index),
                device_id_type=MESH,
            ).wait_recv()
        seconds = []
        for p in range(0, count, 2):
            seconds += spectra([arrived[r, j + i] for i in range(p, min(p + 2, count))], col_ref[...], row_ref[...])
        a, b, c, d = correlate(
            [(firsts[r, j + i, 0], firsts[r, j + i, 1]) for i in range(count)],
            seconds,
            inv_row_ref[...],
            inv_col_ref[...],
        )
        own = r * slots + sides[r] * half + j
        other = r * slots + (1 - sides[r]) * half + j
        return (
            carry
            + row_place(a, own)
            + row_place(c, other)
            + row_place(b, own + entries)
            + row_place(d, other + entries)
        )

    disp = jnp.zeros((1, LANES), F32)
    plan = [(r, j, GROUP) for r in range(rounds) for j in range(0, half, GROUP)]
    plan = plan[:-1] + [(rounds - 1, half - GROUP + i, c) for i, c in LAST]
    stage = 0
    for r, j, count in plan:
        if stage <= stages:
            greet(stage)
            stage += 1
        disp = work(r, j, count, disp)
        if (r, j) == (0, 0):
            for s in range(rounds):
                line_copy(s).wait()
            ids = line[...]
            id_line = jnp.zeros((1, LANES), F32)
            for s in range(rounds):
                theirs = pltpu.roll(lines[s], jnp.where(sides[s] == 0, half, LANES - half), 1)
                in_round = (lane >= s * slots) & (lane < (s + 1) * slots)
                mine = (lane // half) % 2 == sides[s]
                id_line = id_line + jnp.where(in_round, jnp.where(mine, ids, theirs), 0.0)
            disp = disp + pltpu.roll(id_line, 2 * entries, 1)
    while stage <= stages:
        greet(stage)
        stage += 1

    tile_out[...] = disp
    tiles[me] = disp

    def start(i, carry):
        to = i + jnp.where(i >= me, 1, 0)
        pltpu.make_async_remote_copy(
            src_ref=tile_out,
            dst_ref=tiles.at[me],
            send_sem=tile_send,
            recv_sem=tile_recv,
            device_id=(to // groups, to % groups),
            device_id_type=MESH,
        ).start()
        return carry

    lax.fori_loop(0, devices - 1, start, 0)
    for r in range(rounds):
        for j in range(half):
            window_copy(r, j).wait_send()
    everyone = pltpu.make_async_remote_copy(
        src_ref=tiles.at[pl.ds(0, devices - 1)],
        dst_ref=tiles.at[pl.ds(0, devices - 1)],
        send_sem=tile_send,
        recv_sem=tile_recv,
        device_id=neighbours[0],
        device_id_type=MESH,
    )
    everyone.wait_recv()

    pack = LANES // entries
    node = lax.broadcasted_iota(jnp.int32, (NODE_DEV, LANES), 0).astype(F32)
    first_node = (me * NODE_DEV).astype(F32)
    lane = lax.broadcasted_iota(jnp.int32, (1, LANES), 1)
    onehots = []
    values = []
    for g in range(devices // pack):
        parts = [jnp.zeros((1, LANES), F32)] * 3
        for i in range(pack):
            tile = tiles[g * pack + i]
            here = (lane >= i * entries) & (lane < (i + 1) * entries)
            for c in range(3):
                moved = pltpu.roll(tile, ((i - c) * entries) % LANES, 1) if i != c else tile
                parts[c] = jnp.where(here, moved, parts[c])
        onehots.append(jnp.where(parts[2] - first_node == node, 1.0, 0.0).astype(BF16))
        tile = jnp.concatenate(parts[:2], axis=0)
        hi = tile.astype(BF16).astype(F32)
        rest = tile - hi
        mid = rest.astype(BF16).astype(F32)
        values.append(jnp.concatenate([hi, mid, rest - mid, jnp.zeros_like(hi)], axis=0).astype(BF16))
    result = lax.dot_general(
        jnp.concatenate(values, axis=1),
        jnp.concatenate(onehots, axis=1),
        (((1,), (1,)), ((), ())),
        preferred_element_type=F32,
    )
    out_ref[0:2] = result[0:2]
    out_ref[2:4] = result[2:4] + result[4:6]
    everyone.wait_send()


def on_device(strips, edge_colour, patch_offsets, patch_live, node_ids):
    rounds, height, width = strips.shape
    n = PATCH
    slot_count = patch_offsets.shape[2]
    half = slot_count // 2
    devices = lax.axis_size("tiles") * lax.axis_size("grp")
    whole = pl.BlockSpec(memory_space=VMEM)
    anywhere = pl.BlockSpec(memory_space=pl.ANY)
    sem = pltpu.SemaphoreType.DMA
    windows = (rounds, half, n, n)
    scalars = [jnp.transpose(patch_offsets, (0, 1, 3, 2)), edge_colour, patch_live, node_ids]
    constants = [jnp.asarray(t) for t in tables()]
    sums = pl.pallas_call(
        stitch,
        out_shape=jax.ShapeDtypeStruct((4, NODE_DEV), F32),
        in_specs=[pl.BlockSpec(memory_space=SMEM)] * 4 + [anywhere] * 5,
        out_specs=whole,
        scratch_shapes=[
            pltpu.VMEM((rounds, width // LANES, height // SUB, SUB, LANES), BF16),
            *(pltpu.VMEM(t.shape, BF16) for t in constants),
            pltpu.VMEM((PAIR, n + 16, n), F32),
            pltpu.VMEM(windows, BF16),
            pltpu.VMEM((rounds, half, 2, n, n), F32),
            pltpu.VMEM(windows, BF16),
            pltpu.VMEM((1, LANES), F32),
            pltpu.VMEM((rounds, 1, LANES), F32),
            pltpu.VMEM((1, LANES), F32),
            pltpu.VMEM((devices, 1, LANES), F32),
            sem(()),
            sem((4,)),
            sem((rounds, half)),
            sem((rounds, half)),
            sem((rounds,)),
            sem((rounds,)),
            sem(()),
            sem(()),
            pltpu.SemaphoreType.REGULAR((devices.bit_length() - 1,)),
        ],
        compiler_params=pltpu.CompilerParams(collective_id=0, has_side_effects=True, vmem_limit_bytes=VMEM_LIMIT),
        name="stitch",
    )(edge_colour, scalars[0], patch_live, node_ids, strips.reshape(rounds, height // SUB, SUB, width), *constants)
    return sums[0:2] + sums[2:4]


def solution(mesh):
    placed = (
        P(("tiles", "grp"), None, None),
        P(("tiles", "grp"), None),
        P(("tiles", "grp"), None, None, None),
        P(("tiles", "grp"), None),
        P(("tiles", "grp"), None, None),
    )
    return jax.shard_map(
        on_device, mesh=mesh, in_specs=placed, out_specs=P(None, ("tiles", "grp")), check_vma=False
    )
```

time: 34 us -> 35.1 us (1.032)
  Pallas kernels: 32.4 us -> 33.6 us
    pallas_call x2 -> x1, Pallas kernels: 32.4 us -> 33.6 us  [on_device(): pl.pallas_call(stitch, out_shape=jax.ShapeDtypeStruct((4, NODE_DEV), F32)...]
where the time goes in v1:
time: 35.1 us; the launch traced here: 34.9 us
  Pallas kernels  33.6 us (96%)
  other arithmetic  1.32 us (4%)
    pallas_call x1, Pallas kernels, on_device(): pl.pallas_call(stitch, out_shape=jax.ShapeDtypeStruct((4, NODE_DEV), F32)...  33.6 us
    add x1, other arithmetic, on_device(): return sums[0:2] + sums[2:4]  1.32 us

profile of v1, /device:TPU:0, one launch (start us, length us, event | category | flops | bytes accessed | tf_op | source)
XLA Modules:
  0.0 34.9 jit_solution(15773632249669588497)
XLA Ops:
  0.0 33.6 %stitch.1 = f32[4,128]{1,0:T(4,128)} custom-call(s32[1,2]{1,0:T(1,128)} %colour_ref.1, s32[1,2,2,16]{3,2,1,0:T(2,128)} %bitcast.3, s32[1,2]{1,0:T(1,128)} %live_ref.1, s32[1,2,16]{2,1,0:T(2,128)} %ids_ref.1, bf16[2,16,16,4096]{3,2,1,0:T(8,128)(2,1)} %bitcast.2, bf16[256,256]{1,0:T(8,128)(2,1)} %constant.8.clone.col_hbm, ...), custom_call_target="tpu_custom_call" | custom-call | tf_op jit(solution)/shard_map/stitch/pallas_call | solution.py:483
  33.6 1.3 %slice_add_fusion = f32[2,128]{1,0:T(2,128)} fusion(f32[4,128]{1,0:T(4,128)} %stitch.1), kind=kLoop, calls=%fused_computation | loop fusion | flops 256 | bytes 3072 | tf_op jit(solution)/shard_map/add | solution.py:512

commit v2 on v1

--- a/solution.py
+++ b/solution.py
@@ -15,7 +15,7 @@
 GROUP = 4
 PAIR = 2
 SUB = 16
-LAST = ((0, 2), (2, 1), (3, 1))
+LAST = ((0, 4),)
 VMEM_LIMIT = 67043328 - 16384
 
 F32 = jnp.float32
@@ -297,22 +297,21 @@
         for i, window in enumerate(extract(r, [base + j + i for i in range(PAIR)])):
             sent[r, j + i] = window
 
-    order = list(range(rounds))[::-1]
-    produce(order[0], 0)
+    def launch(r, j):
+        for i in range(PAIR):
+            window_copy(r, j + i).start()
+
+    produce(rounds - 1, 0)
     pl.semaphore_wait(barrier, stages)
-    for r in order:
-        if r != order[0]:
-            produce(r, 0)
-            for i in range(PAIR):
-                window_copy(r + 1, half - PAIR + i).start()
-
-        def step(p, carry, r=r):
-            produce(r, p * PAIR)
-            for i in range(PAIR):
-                window_copy(r, (p - 1) * PAIR + i).start()
-            return carry
-
-        lax.fori_loop(1, half // PAIR, step, 0)
+
+    def step(p, carry):
+        for r in reversed(range(rounds)):
+            if r < rounds - 1:
+                produce(r, p * PAIR)
+                launch(r + 1, p * PAIR)
+        produce(rounds - 1, p * PAIR + PAIR)
+        launch(0, p * PAIR)
+        return carry
 
     lane = lax.broadcasted_iota(jnp.int32, (1, LANES), 1)
     ids = jnp.zeros((1, LANES), jnp.int32)
@@ -321,8 +320,16 @@
             node = jnp.where(k < live_ref[0, r], ids_ref[0, r, k], -1)
             ids = jnp.where(lane == r * slots + k, node, ids)
     line[...] = ids.astype(F32)
-    for i in range(PAIR):
-        window_copy(0, half - PAIR + i).start()
+    lax.fori_loop(0, 1, step, 0)
+    for r in range(rounds):
+        line_copy(r).start()
+    last = half - PAIR
+    lax.fori_loop(1, half // PAIR - 1, step, 0)
+    for r in reversed(range(rounds - 1)):
+        produce(r, last)
+        launch(r + 1, last)
+
+    launch(0, last)
     for load in table_loads:
         load.wait()
 
@@ -339,11 +346,7 @@
 
         return step
 
-    lax.fori_loop(0, 1, prepare(0), 0)
     for r in range(rounds):
-        line_copy(r).start()
-    lax.fori_loop(1, half // PAIR, prepare(0), 0)
-    for r in range(1, rounds):
         lax.fori_loop(0, half // PAIR, prepare(r), 0)
 
     def hail(stage):
@@ -393,7 +396,7 @@
             greet(stage)
             stage += 1
         disp = work(r, j, count, disp)
-        if (r, j) == (0, 0):
+        if (r, j) == (rounds - 1, 0):
             for s in range(rounds):
                 line_copy(s).wait()
             ids = line[...]

time: 35.1 us -> 28.8 us (0.82)
  Pallas kernels: 33.6 us -> 27.3 us
    pallas_call x1, Pallas kernels: 33.6 us -> 27.3 us  [on_device(): pl.pallas_call(stitch, out_shape=jax.ShapeDtypeStruct((4, NODE_DEV), F32)...]
where the time goes in v2:
time: 28.8 us; the launch traced here: 28.7 us
  Pallas kernels  27.3 us (95%)
  other arithmetic  1.32 us (5%)
    pallas_call x1, Pallas kernels, on_device(): pl.pallas_call(stitch, out_shape=jax.ShapeDtypeStruct((4, NODE_DEV), F32)...  27.3 us
    add x1, other arithmetic, on_device(): return sums[0:2] + sums[2:4]  1.32 us

profile of v2, /device:TPU:0, one launch (start us, length us, event | category | flops | bytes accessed | tf_op | source)
XLA Modules:
  0.0 28.7 jit_solution(3460378157900899817)
XLA Ops:
  0.0 27.3 %stitch.1 = f32[4,128]{1,0:T(4,128)} custom-call(s32[1,2]{1,0:T(1,128)} %colour_ref.1, s32[1,2,2,16]{3,2,1,0:T(2,128)} %bitcast.3, s32[1,2]{1,0:T(1,128)} %live_ref.1, s32[1,2,16]{2,1,0:T(2,128)} %ids_ref.1, bf16[2,16,16,4096]{3,2,1,0:T(8,128)(2,1)} %bitcast.2, bf16[256,256]{1,0:T(8,128)(2,1)} %constant.8.clone.col_hbm, ...), custom_call_target="tpu_custom_call" | custom-call | tf_op jit(solution)/shard_map/stitch/pallas_call | solution.py:486
  27.3 1.3 %slice_add_fusion = f32[2,128]{1,0:T(2,128)} fusion(f32[4,128]{1,0:T(4,128)} %stitch.1), kind=kLoop, calls=%fused_computation | loop fusion | flops 256 | bytes 3072 | tf_op jit(solution)/shard_map/add | solution.py:515

commit v3 on v2

--- a/solution.py
+++ b/solution.py
@@ -32,20 +32,20 @@
 
 def tables():
     n = PATCH
+    h = n // 2
     j = np.arange(n)
     angle = 2.0 * math.pi / n * ((j[:, None] * j[None, :]) % n)
     c, s = np.cos(angle), np.sin(angle)
-    chi, clo = split_np(np.concatenate([c, s], axis=1))
-    col = np.concatenate([chi, clo], axis=0)
-    rhi, rlo = split_np(np.block([[c, -s], [s, c]]))
-    row = np.concatenate([rhi, rlo, rhi], axis=1)
-    ihi, ilo = split_np(np.concatenate([c, s], axis=1))
-    inv_row = np.concatenate([ihi, ilo, ihi], axis=1)
-    weight = np.where((j == 0) | (j == n // 2), 1.0, 2.0)[:, None]
-    packed = np.where(j[:, None] <= n // 2, weight * c, -2.0 * s) / float(n * n)
-    vhi, vlo = split_np(packed)
-    inv_col = np.concatenate([vhi, vlo, vhi], axis=0)
-    return col, row, inv_row, inv_col
+    rhi, rlo = split_np(np.concatenate([c[: h + 1], s[1:h]], axis=0))
+    fore_row = np.concatenate([rhi, rlo], axis=1)
+    chi, clo = split_np(np.block([[c, -s], [-s, -c]]))
+    fore_col = np.concatenate([chi, clo, chi], axis=0)
+    bhi, blo = split_np(np.block([[c, s], [-s, c]]))
+    back_col = np.concatenate([bhi, blo, bhi], axis=0)
+    weight = np.where(j[:h] == 0, 1.0, 2.0)[None, :]
+    ihi, ilo = split_np(np.concatenate([weight * c[:, :h], c[:, h : h + 1], -2.0 * s[:, 1:h]], axis=1) / float(n * n))
+    back_row = np.concatenate([ihi, ilo, ihi], axis=1)
+    return fore_row, fore_col, back_col, back_row
 
 
 def split(x):
@@ -64,104 +64,141 @@
     return jnp.sum(jnp.where(lane == sub + base, column, 0.0), axis=0, keepdims=True)
 
 
-def spectra(windows, col, row):
+def triple(x):
+    hi, lo = split(x)
+    return jnp.concatenate([hi, hi, lo], axis=1)
+
+
+def gather_rows(rows):
+    sub = lax.broadcasted_iota(jnp.int32, (8, LANES), 0)
+    out = jnp.zeros((8, LANES), F32)
+    for i, row in enumerate(rows):
+        out = jnp.where(sub == i, row, out)
+    return out
+
+
+def spectra(windows, fore_row, fore_col):
     n = PATCH
-    if len(windows) == 1:
-        x = windows[0]
-        hi, lo = split(dot(jnp.concatenate([x, x], axis=1), col))
-        hi, lo = (jnp.concatenate([v[:, :n], v[:, n:]], axis=0) for v in (hi, lo))
-        f = dot(row, jnp.concatenate([hi, hi, lo], axis=0))
-        return [(f[:n], f[n:])]
-    x = jnp.concatenate(windows, axis=0)
-    hi, lo = split(dot(jnp.concatenate([x, x], axis=1), col))
-
-    def stack(v):
-        return jnp.concatenate(
-            [
-                jnp.concatenate([v[:n, :n], v[n:, :n]], axis=1),
-                jnp.concatenate([v[:n, n:], v[n:, n:]], axis=1),
-            ],
-            axis=0,
-        )
-
-    hi, lo = stack(hi), stack(lo)
-    f = dot(row, jnp.concatenate([hi, hi, lo], axis=0))
-    return [(f[:n, :n], f[n:, :n]), (f[:n, n:], f[n:, n:])]
-
-
-def correlate(first, second, inv_row, inv_col):
+    h = n // 2
+    count = len(windows)
+    first = lax.broadcasted_iota(jnp.int32, (8, n), 0) == 0
+    mains = []
+    middles = []
+    for p in range(0, count, 2):
+        x = jnp.concatenate(windows[p : p + 2], axis=1)
+        y = dot(fore_row, jnp.concatenate([x, x], axis=0))
+        for i in range(2):
+            part = y[:, i * n : (i + 1) * n]
+            middles.append(part[h : h + 1])
+            sine = jnp.concatenate([jnp.where(first, 0.0, part[h : h + 8]), part[h + 8 :]], axis=0)
+            mains.append(jnp.concatenate([part[:h], sine], axis=1))
+    middle = gather_rows(middles)
+    mains.append(jnp.concatenate([jnp.concatenate([middle, jnp.zeros_like(middle)], axis=1)] * 2, axis=0))
+    f = dot(jnp.concatenate([triple(m) for m in mains], axis=0), fore_col)
+    main = [(f[i * h : (i + 1) * h, :n], f[i * h : (i + 1) * h, n:]) for i in range(count)]
+    return main, (f[count * h : count * h + 8, :n], f[count * h : count * h + 8, n:])
+
+
+def fold(v):
+    return sum(v[i : i + 8] for i in range(8, v.shape[0], 8)) + v[:8]
+
+
+def whiten_terms(first, second):
+    (r1, i1), (r2, i2) = first, second
+    cross_r = r1 * r2 + i1 * i2
+    cross_i = i1 * r2 - r1 * i2
+    return cross_r, cross_i, jnp.sqrt(cross_r * cross_r + cross_i * cross_i)
+
+
+def total(v):
+    return jnp.sum(v, axis=1, keepdims=True)
+
+
+def correlate(first, second, back_row, back_col):
     n = PATCH
-    count = len(first)
-    lane = lax.broadcasted_iota(jnp.int32, (n, n), 1)
-    low = lane <= n // 2
-    crosses = []
-    mag_sums = []
-    for (r1, i1), (r2, i2) in zip(first, second):
-        cross_r = r1 * r2 + i1 * i2
-        cross_i = r1 * i2 - i1 * r2
-        mag = jnp.sqrt(cross_r * cross_r + cross_i * cross_i)
-        crosses.append((cross_r, cross_i, mag))
-        mag_sums.append(jnp.sum(mag, axis=0, keepdims=True))
-    mean = jnp.sum(jnp.concatenate(mag_sums, axis=0), axis=1, keepdims=True) / float(n * n)
-    extra = 0.1 * mean + 1e-06
+    h = n // 2
+    cells = float(n * n)
+    count = len(first[0])
+    terms = [whiten_terms(a, b) for a, b in zip(first[0], second[0])]
+    middle = whiten_terms(first[1], second[1])
+
+    def spectrum_sum(values, middle_value):
+        folded = jnp.concatenate([jnp.sum(fold(v), axis=0, keepdims=True) for v in values], axis=0)
+        edge = jnp.concatenate([v[:1] for v in values], axis=0)
+        return 2.0 * folded - edge + middle_value[:count], edge
+
+    mag_sum, _ = spectrum_sum([t[2] for t in terms], middle[2])
+    extra = 0.1 * (total(mag_sum) / cells) + 1e-06
+    inverses = [1.0 / (t[2] + extra[p : p + 1]) for p, t in enumerate(terms)]
+    middle_inverse = 1.0 / (middle[2] + gather_rows([extra[p : p + 1] for p in range(count)]))
+    rows = [jnp.concatenate([t[0] * v, t[1] * v], axis=1) for t, v in zip(terms, inverses)]
+    middle_row = jnp.concatenate([middle[0] * middle_inverse, middle[1] * middle_inverse], axis=1)
+    rows.append(jnp.concatenate([middle_row, middle_row], axis=0))
+
+    def power(m, v):
+        return (m * v) * (m * v)
+
+    power_sum, edge = spectrum_sum(
+        [power(t[2], v) for t, v in zip(terms, inverses)], power(middle[2], middle_inverse)
+    )
+    lane = lax.broadcasted_iota(jnp.int32, (count, n), 1)
+    variance = total(power_sum - jnp.where(lane == 0, edge, 0.0)) / (cells * cells)
+    scale = 2.0 / jnp.sqrt(variance + 1e-06) * math.log2(math.e)
+
+    back = dot(jnp.concatenate([triple(r) for r in rows], axis=0), back_col)
+    middle_back = back[count * h : count * h + 8, :n]
+    first_row = lax.broadcasted_iota(jnp.int32, (8, n), 0) == 0
     surfaces = []
-    packed = []
-    sums = []
-    for p in range(count):
-        cross_r, cross_i, mag = crosses[p]
-        inverse = 1.0 / (mag + extra[p : p + 1])
-        g_r = cross_r * inverse
-        g_i = cross_i * inverse
-        packed.append(
-            split(jnp.concatenate([jnp.where(low, g_r, g_i), jnp.where(low, -g_i, g_r)], axis=0))
-        )
-    surfaces_wide = []
     for p in range(0, count, 2):
-        some = packed[p : p + 2]
-        hi = jnp.concatenate([v[0] for v in some], axis=1)
-        lo = jnp.concatenate([v[1] for v in some], axis=1)
-        b = dot(inv_row, jnp.concatenate([hi, hi, lo], axis=0))
-        bhi, blo = split(jnp.concatenate([b[:, i * n : (i + 1) * n] for i in range(len(some))], axis=0))
-        wide = dot(jnp.concatenate([bhi, bhi, blo], axis=1), inv_col)
-        surfaces_wide += [wide[i * n : (i + 1) * n] for i in range(len(some))]
-    for surface in surfaces_wide:
-        surfaces.append(surface)
-        sums.append(jnp.sum(surface, axis=0, keepdims=True))
-    centre = jnp.sum(jnp.concatenate(sums, axis=0), axis=1, keepdims=True) / float(n * n)
-    squares = []
+        columns = []
+        for q in range(p, p + 2):
+            part = back[q * h : (q + 1) * h]
+            imag = part[:, n:]
+            head = jnp.where(first_row, middle_back[q : q + 1], imag[:8])
+            columns.append(jnp.concatenate([part[:, :n], head, imag[8:]], axis=0))
+        hi, lo = split(jnp.concatenate(columns, axis=1))
+        wide = dot(back_row, jnp.concatenate([hi, hi, lo], axis=0))
+        surfaces += [wide[:, :n], wide[:, n:]]
+
     tops = []
-    for p in range(count):
-        deviation = surfaces[p] - centre[p : p + 1]
-        squares.append(jnp.sum(deviation * deviation, axis=0, keepdims=True))
-        tops.append(jnp.max(surfaces[p], axis=0, keepdims=True))
-    variance = jnp.sum(jnp.concatenate(squares, axis=0), axis=1, keepdims=True) / float(n * n)
+    for surface in surfaces:
+        peak = surface[:8]
+        for i in range(8, n, 8):
+            peak = jnp.maximum(peak, surface[i : i + 8])
+        tops.append(jnp.max(peak, axis=0, keepdims=True))
     top = jnp.max(jnp.concatenate(tops, axis=0), axis=1, keepdims=True)
-    scale = 2.0 / jnp.sqrt(variance + 1e-06)
-    sub = lax.broadcasted_iota(jnp.int32, (n, n), 0)
-    sub_coord = ((sub + n // 2) % n - n // 2).astype(F32)
+    sub = lax.broadcasted_iota(jnp.int32, (8, n), 0).astype(F32)
     columns = []
     rows = []
     edges = []
     for p in range(count):
-        e = jnp.exp((surfaces[p] - top[p : p + 1]) * scale[p : p + 1])
-        columns.append(jnp.sum(e, axis=0, keepdims=True))
-        rows.append(jnp.sum(e * sub_coord, axis=0, keepdims=True))
-        edges.append(e[n // 2 : n // 2 + 1, :])
+        e = jnp.exp2((surfaces[p] - top[p : p + 1]) * scale[p : p + 1])
+        part = [e[i : i + 8] for i in range(0, n, 8)]
+        upper = part[h // 8 - 1]
+        step = upper
+        for v in part[h // 8 - 2 : 0 : -1]:
+            upper = upper + v
+            step = step + upper
+        upper = upper + part[0]
+        lower = part[h // 8]
+        down = lower
+        for v in part[h // 8 + 1 :]:
+            lower = lower + v
+            down = down + lower
+        column = upper + lower
+        columns.append(jnp.sum(column, axis=0, keepdims=True))
+        rows.append(jnp.sum(8.0 * (step - down) + sub * column, axis=0, keepdims=True))
+        edges.append(e[h : h + 1, :])
     columns = jnp.concatenate(columns, axis=0)
     rows = jnp.concatenate(rows, axis=0)
     edges = jnp.concatenate(edges, axis=0)
-    lane = lax.broadcasted_iota(jnp.int32, (count, n), 1)
-    lane_coord = ((lane + n // 2) % n - n // 2).astype(F32)
-
-    def total(v):
-        return jnp.sum(v, axis=1, keepdims=True)
-
+    lane_coord = ((lane + h) % n - h).astype(F32)
     unit = float(n // 8)
     norm = 1.0 / total(columns)
     row_shift = total(rows) * norm / unit
     col_shift = total(columns * lane_coord) * norm / unit
     row_edge = total(edges) * norm * (float(n) / unit)
-    col_edge = total(jnp.where(lane == n // 2, columns, 0.0)) * norm * (float(n) / unit)
+    col_edge = total(jnp.where(lane == h, columns, 0.0)) * norm * (float(n) / unit)
     return row_shift, col_shift, -row_shift - row_edge, -col_shift - col_edge
 
 
@@ -174,19 +211,20 @@
     live_ref,
     ids_ref,
     strips_hbm,
-    col_hbm,
-    row_hbm,
-    inv_row_hbm,
-    inv_col_hbm,
+    fore_row_hbm,
+    fore_col_hbm,
+    back_col_hbm,
+    back_row_hbm,
     out_ref,
     strips,
-    col_ref,
-    row_ref,
-    inv_row_ref,
-    inv_col_ref,
+    fore_row_ref,
+    fore_col_ref,
+    back_col_ref,
+    back_row_ref,
     shifted,
     sent,
     firsts,
+    middles,
     arrived,
     line,
     lines,
@@ -242,7 +280,7 @@
     table_loads = [
         pltpu.make_async_copy(a, b, table_sem.at[i])
         for i, (a, b) in enumerate(
-            [(col_hbm, col_ref), (row_hbm, row_ref), (inv_row_hbm, inv_row_ref), (inv_col_hbm, inv_col_ref)]
+            [(fore_row_hbm, fore_row_ref), (fore_col_hbm, fore_col_ref), (back_col_hbm, back_col_ref), (back_row_hbm, back_row_ref)]
         )
     ]
     for load in table_loads:
@@ -334,20 +372,20 @@
         load.wait()
 
     def prepare(r):
-        def step(p, carry):
-            j = p * PAIR
-            windows = extract(r, [sides[r] * half + j + i for i in range(PAIR)])
-            for q in range(0, PAIR, 2):
-                pair = spectra(windows[q : q + 2], col_ref[...], row_ref[...])
-                for i in range(2):
-                    for c in range(2):
-                        firsts[r, j + q + i, c] = pair[i][c]
+        def step(g, carry):
+            j = g * GROUP
+            windows = extract(r, [sides[r] * half + j + i for i in range(GROUP)])
+            main, middle = spectra(windows, fore_row_ref[...], fore_col_ref[...])
+            for c in range(2):
+                for i in range(GROUP):
+                    firsts[r, j + i, c] = main[i][c]
+                middles[r, g, c] = middle[c]
             return carry
 
         return step
 
     for r in range(rounds):
-        lax.fori_loop(0, half // PAIR, prepare(r), 0)
+        lax.fori_loop(0, half // GROUP, prepare(r), 0)
 
     def hail(stage):
         pl.semaphore_signal(hello.at[stage], inc=1, device_id=neighbours[stage], device_id_type=MESH)
@@ -368,14 +406,13 @@
                 device_id=(partners[r], group_index),
                 device_id_type=MESH,
             ).wait_recv()
-        seconds = []
-        for p in range(0, count, 2):
-            seconds += spectra([arrived[r, j + i] for i in range(p, min(p + 2, count))], col_ref[...], row_ref[...])
+        g = j // GROUP
+        seconds = spectra([arrived[r, j + i] for i in range(count)], fore_row_ref[...], fore_col_ref[...])
         a, b, c, d = correlate(
-            [(firsts[r, j + i, 0], firsts[r, j + i, 1]) for i in range(count)],
+            ([(firsts[r, j + i, 0], firsts[r, j + i, 1]) for i in range(count)], (middles[r, g, 0], middles[r, g, 1])),
             seconds,
-            inv_row_ref[...],
-            inv_col_ref[...],
+            back_row_ref[...],
+            back_col_ref[...],
         )
         own = r * slots + sides[r] * half + j
         other = r * slots + (1 - sides[r]) * half + j
@@ -491,9 +528,10 @@
         scratch_shapes=[
             pltpu.VMEM((rounds, width // LANES, height // SUB, SUB, LANES), BF16),
             *(pltpu.VMEM(t.shape, BF16) for t in constants),
-            pltpu.VMEM((PAIR, n + 16, n), F32),
+            pltpu.VMEM((GROUP, n + 16, n), F32),
             pltpu.VMEM(windows, BF16),
-            pltpu.VMEM((rounds, half, 2, n, n), F32),
+            pltpu.VMEM((rounds, half, 2, n // 2, n), F32),
+            pltpu.VMEM((rounds, half // GROUP, 2, 8, n), F32),
             pltpu.VMEM(windows, BF16),
             pltpu.VMEM((1, LANES), F32),
             pltpu.VMEM((rounds, 1, LANES), F32),

time: 28.8 us -> 28.4 us (0.986)
  Pallas kernels: 27.3 us -> 26.8 us
    pallas_call x1, Pallas kernels: 27.3 us -> 26.8 us  [on_device(): pl.pallas_call(stitch, out_shape=jax.ShapeDtypeStruct((4, NODE_DEV), F32)...]
where the time goes in v3:
time: 28.4 us; the launch traced here: 28.2 us
  Pallas kernels  26.8 us (94%)
  other arithmetic  1.32 us (5%)
    pallas_call x1, Pallas kernels, on_device(): pl.pallas_call(stitch, out_shape=jax.ShapeDtypeStruct((4, NODE_DEV), F32)...  26.8 us
    add x1, other arithmetic, on_device(): return sums[0:2] + sums[2:4]  1.32 us

profile of v3, /device:TPU:0, one launch (start us, length us, event | category | flops | bytes accessed | tf_op | source)
XLA Modules:
  0.0 28.2 jit_solution(14292096684863788591)
XLA Ops:
  0.0 26.8 %stitch.1 = f32[4,128]{1,0:T(4,128)} custom-call(s32[1,2]{1,0:T(1,128)} %colour_ref.1, s32[1,2,2,16]{3,2,1,0:T(2,128)} %bitcast.3, s32[1,2]{1,0:T(1,128)} %live_ref.1, s32[1,2,16]{2,1,0:T(2,128)} %ids_ref.1, bf16[2,16,16,4096]{3,2,1,0:T(8,128)(2,1)} %bitcast.2, bf16[128,256]{1,0:T(8,128)(2,1)} %constant.8.clone.fore_row_hbm, ...), custom_call_target="tpu_custom_call" | custom-call | tf_op jit(solution)/shard_map/stitch/pallas_call | solution.py:523
  26.9 1.3 %slice_add_fusion = f32[2,128]{1,0:T(2,128)} fusion(f32[4,128]{1,0:T(4,128)} %stitch.1), kind=kLoop, calls=%fused_computation | loop fusion | flops 256 | bytes 3072 | tf_op jit(solution)/shard_map/add | solution.py:553

commit v4 on v3

--- a/solution.py
+++ b/solution.py
@@ -14,8 +14,8 @@
 LANES = 128
 GROUP = 4
 PAIR = 2
-SUB = 16
-LAST = ((0, 4),)
+SUB = 8
+DOT = 2
 VMEM_LIMIT = 67043328 - 16384
 
 F32 = jnp.float32
@@ -67,6 +67,19 @@
 def triple(x):
     hi, lo = split(x)
     return jnp.concatenate([hi, hi, lo], axis=1)
+
+
+def apply(rows, table):
+    out = []
+    for p in range(0, len(rows), DOT):
+        some = rows[p : p + DOT] if len(rows) - p > DOT + 1 else rows[p:]
+        y = dot(jnp.concatenate([triple(v) for v in some], axis=0), table)
+        at = 0
+        for v in some:
+            out.append(y[at : at + v.shape[0]])
+            at += v.shape[0]
+        if p + len(some) == len(rows):
+            return out
 
 
 def gather_rows(rows):
@@ -94,9 +107,9 @@
             mains.append(jnp.concatenate([part[:h], sine], axis=1))
     middle = gather_rows(middles)
     mains.append(jnp.concatenate([jnp.concatenate([middle, jnp.zeros_like(middle)], axis=1)] * 2, axis=0))
-    f = dot(jnp.concatenate([triple(m) for m in mains], axis=0), fore_col)
-    main = [(f[i * h : (i + 1) * h, :n], f[i * h : (i + 1) * h, n:]) for i in range(count)]
-    return main, (f[count * h : count * h + 8, :n], f[count * h : count * h + 8, n:])
+    parts = apply(mains, fore_col)
+    main = [(f[:, :n], f[:, n:]) for f in parts[:-1]]
+    return main, (parts[-1][:8, :n], parts[-1][:8, n:])
 
 
 def fold(v):
@@ -145,14 +158,14 @@
     variance = total(power_sum - jnp.where(lane == 0, edge, 0.0)) / (cells * cells)
     scale = 2.0 / jnp.sqrt(variance + 1e-06) * math.log2(math.e)
 
-    back = dot(jnp.concatenate([triple(r) for r in rows], axis=0), back_col)
-    middle_back = back[count * h : count * h + 8, :n]
+    back = apply(rows, back_col)
+    middle_back = back[-1][:8, :n]
     first_row = lax.broadcasted_iota(jnp.int32, (8, n), 0) == 0
     surfaces = []
     for p in range(0, count, 2):
         columns = []
         for q in range(p, p + 2):
-            part = back[q * h : (q + 1) * h]
+            part = back[q]
             imag = part[:, n:]
             head = jnp.where(first_row, middle_back[q : q + 1], imag[:8])
             columns.append(jnp.concatenate([part[:, :n], head, imag[8:]], axis=0))
@@ -206,16 +219,20 @@
 
 
 def stitch(
-    colour_ref,
-    offset_ref,
-    live_ref,
-    ids_ref,
+    colour_hbm,
+    offset_hbm,
+    live_hbm,
+    ids_hbm,
     strips_hbm,
     fore_row_hbm,
     fore_col_hbm,
     back_col_hbm,
     back_row_hbm,
     out_ref,
+    colour_ref,
+    offset_ref,
+    live_ref,
+    ids_ref,
     strips,
     fore_row_ref,
     fore_col_ref,
@@ -230,6 +247,7 @@
     lines,
     tile_out,
     tiles,
+    scalar_sem,
     strip_sem,
     table_sem,
     window_send,
@@ -241,7 +259,7 @@
     hello,
 ):
     n = PATCH
-    rounds, blocks, layers = strips.shape[:3]
+    rounds, layers, blocks = strips.shape[:3]
     slots = offset_ref.shape[3]
     half = slots // 2
     entries = rounds * slots
@@ -271,10 +289,15 @@
     for at in neighbours:
         pl.semaphore_signal(barrier, inc=1, device_id=at, device_id_type=MESH)
 
-    strip_loads = [
-        pltpu.make_async_copy(strips_hbm.at[:, :, :, pl.ds(i * LANES, LANES)], strips.at[:, i], strip_sem)
-        for i in range(blocks)
+    scalar_loads = [
+        pltpu.make_async_copy(a, b, scalar_sem.at[i])
+        for i, (a, b) in enumerate(
+            [(offset_hbm, offset_ref), (colour_hbm, colour_ref), (live_hbm, live_ref), (ids_hbm, ids_ref)]
+        )
     ]
+    for load in scalar_loads:
+        load.start()
+    strip_loads = [pltpu.make_async_copy(strips_hbm.at[r], strips.at[r], strip_sem.at[r]) for r in range(rounds)]
     for load in strip_loads:
         load.start()
     table_loads = [
@@ -285,8 +308,6 @@
     ]
     for load in table_loads:
         load.start()
-    pltpu.make_async_copy(strips, strips, strip_sem).wait()
-
     def extract(r, picks):
         rests = []
         lane = lax.broadcasted_iota(jnp.int32, (n + SUB, LANES), 1)
@@ -298,7 +319,7 @@
             turn = lax.rem(2 * LANES - shift, LANES)
             left, right = (
                 pltpu.roll(
-                    strips[colour_ref[0, r], block + side, pl.ds(layer, n // SUB + 1)]
+                    strips[colour_ref[0, r], pl.ds(layer, n // SUB + 1), block + side]
                     .reshape(n + SUB, LANES)
                     .astype(F32),
                     turn,
@@ -310,13 +331,19 @@
             rests.append(row - layer * SUB)
         return [shifted[i, pl.ds(rest, n), :].astype(BF16) for i, rest in enumerate(rests)]
 
+    def pick(r, values):
+        value = values[0]
+        for i in range(1, rounds):
+            value = jnp.where(r == i, values[i], value)
+        return value
+
     def window_copy(r, j):
         return pltpu.make_async_remote_copy(
             src_ref=sent.at[r, j],
             dst_ref=arrived.at[r, j],
             send_sem=window_send.at[r, j],
             recv_sem=window_recv.at[r, j],
-            device_id=(partners[r], group_index),
+            device_id=(pick(r, partners), group_index),
             device_id_type=MESH,
         )
 
@@ -330,123 +357,108 @@
             device_id_type=MESH,
         )
 
-    def produce(r, j):
-        base = (1 - sides[r]) * half
-        for i, window in enumerate(extract(r, [base + j + i for i in range(PAIR)])):
-            sent[r, j + i] = window
-
-    def launch(r, j):
+    for load in scalar_loads:
+        load.wait()
+    lane = lax.broadcasted_iota(jnp.int32, (1, LANES), 1)
+
+    def place_id(i, ids):
+        r, k = i // slots, i % slots
+        return jnp.where(lane == i, jnp.where(k < live_ref[0, r], ids_ref[0, r, k], -1), ids)
+
+    line[...] = lax.fori_loop(0, entries, place_id, jnp.zeros((1, LANES), jnp.int32)).astype(F32)
+    for load in strip_loads:
+        load.wait()
+    pl.semaphore_wait(barrier, stages)
+    for r in range(rounds):
+        line_copy(r).start()
+
+    def place_of(q):
+        return rounds - 1 - q % rounds, (q // rounds) * PAIR
+
+    def launch(q):
+        r, j = place_of(q)
         for i in range(PAIR):
             window_copy(r, j + i).start()
 
-    produce(rounds - 1, 0)
-    pl.semaphore_wait(barrier, stages)
-
-    def step(p, carry):
-        for r in reversed(range(rounds)):
-            if r < rounds - 1:
-                produce(r, p * PAIR)
-                launch(r + 1, p * PAIR)
-        produce(rounds - 1, p * PAIR + PAIR)
-        launch(0, p * PAIR)
+    def produce(q, carry):
+        r, j = place_of(q)
+        base = (1 - pick(r, sides)) * half + j
+        for i, window in enumerate(extract(r, [base + i for i in range(PAIR)])):
+            sent[r, j + i] = window
+
+        @pl.when(q > 0)
+        def _():
+            launch(q - 1)
+
         return carry
 
-    lane = lax.broadcasted_iota(jnp.int32, (1, LANES), 1)
-    ids = jnp.zeros((1, LANES), jnp.int32)
-    for r in range(rounds):
-        for k in range(slots):
-            node = jnp.where(k < live_ref[0, r], ids_ref[0, r, k], -1)
-            ids = jnp.where(lane == r * slots + k, node, ids)
-    line[...] = ids.astype(F32)
-    lax.fori_loop(0, 1, step, 0)
-    for r in range(rounds):
-        line_copy(r).start()
-    last = half - PAIR
-    lax.fori_loop(1, half // PAIR - 1, step, 0)
-    for r in reversed(range(rounds - 1)):
-        produce(r, last)
-        launch(r + 1, last)
-
-    launch(0, last)
+    lax.fori_loop(0, rounds * half // PAIR, produce, 0)
     for load in table_loads:
         load.wait()
-
-    def prepare(r):
-        def step(g, carry):
-            j = g * GROUP
-            windows = extract(r, [sides[r] * half + j + i for i in range(GROUP)])
-            main, middle = spectra(windows, fore_row_ref[...], fore_col_ref[...])
-            for c in range(2):
-                for i in range(GROUP):
-                    firsts[r, j + i, c] = main[i][c]
-                middles[r, g, c] = middle[c]
-            return carry
-
-        return step
-
-    for r in range(rounds):
-        lax.fori_loop(0, half // GROUP, prepare(r), 0)
+    launch(rounds * half // PAIR - 1)
+    parts = half // GROUP
+
+    def prepare(g, carry):
+        r, part = g // parts, g % parts
+        j = part * GROUP
+        windows = extract(r, [pick(r, sides) * half + j + i for i in range(GROUP)])
+        main, middle = spectra(windows, fore_row_ref[...], fore_col_ref[...])
+        for c in range(2):
+            for i in range(GROUP):
+                firsts[r, j + i, c] = main[i][c]
+            middles[r, part, c] = middle[c]
+        return carry
+
+    lax.fori_loop(0, rounds * parts, prepare, 0)
+
+    def neighbour(stage):
+        tile, group = neighbours[0]
+        for i in range(1, stages):
+            tile = jnp.where(stage == i, neighbours[i][0], tile)
+            group = jnp.where(stage == i, neighbours[i][1], group)
+        return tile, group
 
     def hail(stage):
-        pl.semaphore_signal(hello.at[stage], inc=1, device_id=neighbours[stage], device_id_type=MESH)
-
-    def greet(stage):
-        if stage > 0:
-            pl.semaphore_wait(hello.at[stage - 1], 1)
-        if stage < stages:
-            hail(stage)
-
-    def work(r, j, count, carry):
-        for i in range(count):
-            pltpu.make_async_remote_copy(
-                src_ref=sent.at[r, j + i],
-                dst_ref=arrived.at[r, j + i],
-                send_sem=window_send.at[r, j + i],
-                recv_sem=window_recv.at[r, j + i],
-                device_id=(partners[r], group_index),
-                device_id_type=MESH,
-            ).wait_recv()
-        g = j // GROUP
-        seconds = spectra([arrived[r, j + i] for i in range(count)], fore_row_ref[...], fore_col_ref[...])
+        pl.semaphore_signal(hello.at[stage], inc=1, device_id=neighbour(stage), device_id_type=MESH)
+
+    def work(g, disp):
+        r, part = g // parts, g % parts
+        j = part * GROUP
+        hail(early + g)
+        for i in range(GROUP):
+            window_copy(r, j + i).wait_recv()
+        seconds = spectra([arrived[r, j + i] for i in range(GROUP)], fore_row_ref[...], fore_col_ref[...])
         a, b, c, d = correlate(
-            ([(firsts[r, j + i, 0], firsts[r, j + i, 1]) for i in range(count)], (middles[r, g, 0], middles[r, g, 1])),
+            ([(firsts[r, j + i, 0], firsts[r, j + i, 1]) for i in range(GROUP)], (middles[r, part, 0], middles[r, part, 1])),
             seconds,
             back_row_ref[...],
             back_col_ref[...],
         )
-        own = r * slots + sides[r] * half + j
-        other = r * slots + (1 - sides[r]) * half + j
+        own = r * slots + pick(r, sides) * half + j
+        other = r * slots + (1 - pick(r, sides)) * half + j
+        pl.semaphore_wait(hello.at[early + g], 1)
         return (
-            carry
+            disp
             + row_place(a, own)
             + row_place(c, other)
             + row_place(b, own + entries)
             + row_place(d, other + entries)
         )
 
-    disp = jnp.zeros((1, LANES), F32)
-    plan = [(r, j, GROUP) for r in range(rounds) for j in range(0, half, GROUP)]
-    plan = plan[:-1] + [(rounds - 1, half - GROUP + i, c) for i, c in LAST]
-    stage = 0
-    for r, j, count in plan:
-        if stage <= stages:
-            greet(stage)
-            stage += 1
-        disp = work(r, j, count, disp)
-        if (r, j) == (rounds - 1, 0):
-            for s in range(rounds):
-                line_copy(s).wait()
-            ids = line[...]
-            id_line = jnp.zeros((1, LANES), F32)
-            for s in range(rounds):
-                theirs = pltpu.roll(lines[s], jnp.where(sides[s] == 0, half, LANES - half), 1)
-                in_round = (lane >= s * slots) & (lane < (s + 1) * slots)
-                mine = (lane // half) % 2 == sides[s]
-                id_line = id_line + jnp.where(in_round, jnp.where(mine, ids, theirs), 0.0)
-            disp = disp + pltpu.roll(id_line, 2 * entries, 1)
-    while stage <= stages:
-        greet(stage)
-        stage += 1
+    early = stages - rounds * parts
+    for i in range(early):
+        hail(i)
+        pl.semaphore_wait(hello.at[i], 1)
+    for s in range(rounds):
+        line_copy(s).wait()
+    ids = line[...]
+    id_line = jnp.zeros((1, LANES), F32)
+    for s in range(rounds):
+        theirs = pltpu.roll(lines[s], jnp.where(sides[s] == 0, half, LANES - half), 1)
+        in_round = (lane >= s * slots) & (lane < (s + 1) * slots)
+        mine = (lane // half) % 2 == sides[s]
+        id_line = id_line + jnp.where(in_round, jnp.where(mine, ids, theirs), 0.0)
+    disp = lax.fori_loop(0, rounds * parts, work, pltpu.roll(id_line, 2 * entries, 1))
 
     tile_out[...] = disp
     tiles[me] = disp
@@ -464,9 +476,12 @@
         return carry
 
     lax.fori_loop(0, devices - 1, start, 0)
-    for r in range(rounds):
-        for j in range(half):
-            window_copy(r, j).wait_send()
+
+    def drain(i, carry):
+        window_copy(i // half, i % half).wait_send()
+        return carry
+
+    lax.fori_loop(0, rounds * half, drain, 0)
     everyone = pltpu.make_async_remote_copy(
         src_ref=tiles.at[pl.ds(0, devices - 1)],
         dst_ref=tiles.at[pl.ds(0, devices - 1)],
@@ -518,17 +533,22 @@
     anywhere = pl.BlockSpec(memory_space=pl.ANY)
     sem = pltpu.SemaphoreType.DMA
     windows = (rounds, half, n, n)
+    tiled = strips.reshape(rounds, height // SUB, SUB, width // LANES, LANES).transpose(0, 1, 3, 2, 4)
     scalars = [jnp.transpose(patch_offsets, (0, 1, 3, 2)), edge_colour, patch_live, node_ids]
     constants = [jnp.asarray(t) for t in tables()]
     sums = pl.pallas_call(
         stitch,
         out_shape=jax.ShapeDtypeStruct((4, NODE_DEV), F32),
-        in_specs=[pl.BlockSpec(memory_space=SMEM)] * 4 + [anywhere] * 5,
+        in_specs=[anywhere] * 9,
         out_specs=whole,
         scratch_shapes=[
-            pltpu.VMEM((rounds, width // LANES, height // SUB, SUB, LANES), BF16),
+            pltpu.SMEM(edge_colour.shape, jnp.int32),
+            pltpu.SMEM(scalars[0].shape, jnp.int32),
+            pltpu.SMEM(patch_live.shape, jnp.int32),
+            pltpu.SMEM(node_ids.shape, jnp.int32),
+            pltpu.VMEM(tiled.shape, BF16),
             *(pltpu.VMEM(t.shape, BF16) for t in constants),
-            pltpu.VMEM((GROUP, n + 16, n), F32),
+            pltpu.VMEM((GROUP, n + SUB, n), F32),
             pltpu.VMEM(windows, BF16),
             pltpu.VMEM((rounds, half, 2, n // 2, n), F32),
             pltpu.VMEM((rounds, half // GROUP, 2, 8, n), F32),
@@ -537,7 +557,8 @@
             pltpu.VMEM((rounds, 1, LANES), F32),
             pltpu.VMEM((1, LANES), F32),
             pltpu.VMEM((devices, 1, LANES), F32),
-            sem(()),
+            sem((4,)),
+            sem((rounds,)),
             sem((4,)),
             sem((rounds, half)),
             sem((rounds, half)),
@@ -549,7 +570,7 @@
         ],
         compiler_params=pltpu.CompilerParams(collective_id=0, has_side_effects=True, vmem_limit_bytes=VMEM_LIMIT),
         name="stitch",
-    )(edge_colour, scalars[0], patch_live, node_ids, strips.reshape(rounds, height // SUB, SUB, width), *constants)
+    )(edge_colour, scalars[0], patch_live, node_ids, tiled, *constants)
     return sums[0:2] + sums[2:4]
 
 

time: 28.4 us -> 27.6 us (0.972)
  Pallas kernels: 26.8 us -> 26.1 us
    pallas_call x1, Pallas kernels: 26.8 us -> 26.1 us  [on_device(): pl.pallas_call(stitch, out_shape=jax.ShapeDtypeStruct((4, NODE_DEV), F32)...]
where the time goes in v4:
time: 27.6 us; the launch traced here: 27.4 us
  Pallas kernels  26.1 us (95%)
  other arithmetic  1.32 us (5%)
    pallas_call x1, Pallas kernels, on_device(): pl.pallas_call(stitch, out_shape=jax.ShapeDtypeStruct((4, NODE_DEV), F32)...  26.1 us
    add x1, other arithmetic, on_device(): return sums[0:2] + sums[2:4]  1.32 us

profile of v4, /device:TPU:0, one launch (start us, length us, event | category | flops | bytes accessed | tf_op | source)
XLA Modules:
  0.0 27.4 jit_solution(1316740002498119700)
XLA Ops:
  0.0 26.1 %stitch.1 = f32[4,128]{1,0:T(4,128)} custom-call(s32[1,2]{1,0:T(1,128)} %colour_hbm.1, s32[1,2,2,16]{3,2,1,0:T(2,128)} %bitcast.5, s32[1,2]{1,0:T(1,128)} %live_hbm.1, s32[1,2,16]{2,1,0:T(2,128)} %ids_hbm.1, bf16[2,32,32,8,128]{4,3,2,1,0:T(8,128)(2,1)} %bitcast.4, bf16[128,256]{1,0:T(8,128)(2,1)} %constant.8.clone.fore_row_hbm, ...), custom_call_target="tpu_custom_call" | custom-call | tf_op jit(solution)/shard_map/stitch/pallas_call | solution.py:539
  26.1 1.3 %slice_add_fusion = f32[2,128]{1,0:T(2,128)} fusion(f32[4,128]{1,0:T(4,128)} %stitch.1), kind=kLoop, calls=%fused_computation | loop fusion | flops 256 | bytes 3072 | tf_op jit(solution)/shard_map/add | solution.py:574

commit v5 on v4

--- a/solution.py
+++ b/solution.py
@@ -16,7 +16,7 @@
 PAIR = 2
 SUB = 8
 DOT = 2
-VMEM_LIMIT = 67043328 - 16384
+VMEM_LIMIT = 32 * 1024 * 1024
 
 F32 = jnp.float32
 BF16 = jnp.bfloat16
@@ -518,8 +518,7 @@
         (((1,), (1,)), ((), ())),
         preferred_element_type=F32,
     )
-    out_ref[0:2] = result[0:2]
-    out_ref[2:4] = result[2:4] + result[4:6]
+    out_ref[...] = result[0:2] + (result[2:4] + result[4:6])
     everyone.wait_send()
 
 
@@ -530,7 +529,7 @@
     half = slot_count // 2
     devices = lax.axis_size("tiles") * lax.axis_size("grp")
     whole = pl.BlockSpec(memory_space=VMEM)
-    anywhere = pl.BlockSpec(memory_space=pl.ANY)
+    anywhere = pl.BlockSpec(memory_space=pltpu.MemorySpace.HBM)
     sem = pltpu.SemaphoreType.DMA
     windows = (rounds, half, n, n)
     tiled = strips.reshape(rounds, height // SUB, SUB, width // LANES, LANES).transpose(0, 1, 3, 2, 4)
@@ -538,7 +537,7 @@
     constants = [jnp.asarray(t) for t in tables()]
     sums = pl.pallas_call(
         stitch,
-        out_shape=jax.ShapeDtypeStruct((4, NODE_DEV), F32),
+        out_shape=jax.ShapeDtypeStruct((2, NODE_DEV), F32),
         in_specs=[anywhere] * 9,
         out_specs=whole,
         scratch_shapes=[
@@ -570,8 +569,8 @@
         ],
         compiler_params=pltpu.CompilerParams(collective_id=0, has_side_effects=True, vmem_limit_bytes=VMEM_LIMIT),
         name="stitch",
-    )(edge_colour, scalars[0], patch_live, node_ids, tiled, *constants)
-    return sums[0:2] + sums[2:4]
+    )(*(pltpu.with_memory_space_constraint(v, pltpu.MemorySpace.HBM) for v in (edge_colour, scalars[0], patch_live, node_ids, tiled, *constants)))
+    return sums
 
 
 def solution(mesh):

time: 27.6 us -> 26.2 us (0.949)
  other arithmetic: 1.32 us -> 0 us
  Pallas kernels: 26.1 us -> 25.5 us
  local copies, waits for them, and re-layouts: 0 us -> 0.56 us
    add x1 -> x0, other arithmetic: 1.32 us -> none  [on_device(): return sums[0:2] + sums[2:4]]
    pallas_call x1, Pallas kernels: 26.1 us -> 25.5 us  [on_device(): pl.pallas_call(stitch, out_shape=jax.ShapeDtypeStruct((2, NODE_DEV), F32)...]
    unnamed x0 -> x1, local copies, waits for them, and re-layouts: none -> 0.56 us
where the time goes in v5:
time: 26.2 us; the launch traced here: 26.1 us
  Pallas kernels  25.5 us (97%)
  local copies, waits for them, and re-layouts  0.56 us (2%)
    pallas_call x1, Pallas kernels, on_device(): pl.pallas_call(stitch, out_shape=jax.ShapeDtypeStruct((2, NODE_DEV), F32)...  25.5 us
    unnamed x1, local copies, waits for them, and re-layouts  0.56 us

profile of v5, /device:TPU:0, one launch (start us, length us, event | category | flops | bytes accessed | tf_op | source)
XLA Modules:
  0.0 26.1 jit_solution(8336410712155054368)
XLA Ops:
  0.0 25.5 %stitch.1 = f32[2,128]{1,0:T(2,128)S(1)} custom-call(s32[1,2]{1,0:T(1,128)} %colour_hbm.1, s32[1,2,2,16]{3,2,1,0:T(2,128)} %bitcast.5, s32[1,2]{1,0:T(1,128)} %live_hbm.1, s32[1,2,16]{2,1,0:T(2,128)} %ids_hbm.1, bf16[2,32,32,8,128]{4,3,2,1,0:T(8,128)(2,1)} %bitcast.4, bf16[128,256]{1,0:T(8,128)(2,1)} %constant.8.clone.fore_row_hbm, ...), custom_call_target="tpu_custom_call" | custom-call | tf_op jit(solution)/shard_map/stitch/pallas_call | solution.py:538
  25.5 0.6 %copy.11 = f32[2,128]{1,0:T(2,128)} copy(f32[2,128]{1,0:T(2,128)S(1)} %stitch.1) | data formatting | bytes 2048

commit v6 on v5

--- a/solution.py
+++ b/solution.py
@@ -14,8 +14,11 @@
 LANES = 128
 GROUP = 4
 PAIR = 2
+CUTS = 2
 SUB = 8
 DOT = 2
+LATE = (0,)
+LATE_STEP = 1
 VMEM_LIMIT = 32 * 1024 * 1024
 
 F32 = jnp.float32
@@ -297,7 +300,11 @@
     ]
     for load in scalar_loads:
         load.start()
-    strip_loads = [pltpu.make_async_copy(strips_hbm.at[r], strips.at[r], strip_sem.at[r]) for r in range(rounds)]
+    strip_loads = [
+        pltpu.make_async_copy(strips_hbm.at[r, pl.ds(i, layers // CUTS)], strips.at[r, pl.ds(i, layers // CUTS)], strip_sem.at[r, c])
+        for r in range(rounds)
+        for c, i in enumerate(range(0, layers, layers // CUTS))
+    ]
     for load in strip_loads:
         load.start()
     table_loads = [
@@ -306,8 +313,6 @@
             [(fore_row_hbm, fore_row_ref), (fore_col_hbm, fore_col_ref), (back_col_hbm, back_col_ref), (back_row_hbm, back_row_ref)]
         )
     ]
-    for load in table_loads:
-        load.start()
     def extract(r, picks):
         rests = []
         lane = lax.broadcasted_iota(jnp.int32, (n + SUB, LANES), 1)
@@ -368,6 +373,8 @@
     line[...] = lax.fori_loop(0, entries, place_id, jnp.zeros((1, LANES), jnp.int32)).astype(F32)
     for load in strip_loads:
         load.wait()
+    for load in table_loads:
+        load.start()
     pl.semaphore_wait(barrier, stages)
     for r in range(rounds):
         line_copy(r).start()
@@ -386,12 +393,14 @@
         for i, window in enumerate(extract(r, [base + i for i in range(PAIR)])):
             sent[r, j + i] = window
 
-        @pl.when(q > 0)
+        @pl.when((q > 0) & ((place_of(q - 1)[0] < rounds - 1) | jnp.logical_not(late)))
         def _():
             launch(q - 1)
 
         return carry
 
+    quarter = tile_index // (tile_count // 4)
+    late = functools.reduce(jnp.logical_or, [quarter == v for v in LATE])
     lax.fori_loop(0, rounds * half // PAIR, produce, 0)
     for load in table_loads:
         load.wait()
@@ -424,7 +433,19 @@
     def work(g, disp):
         r, part = g // parts, g % parts
         j = part * GROUP
-        hail(early + g)
+
+        @pl.when(late & (g == LATE_STEP))
+        def _():
+            def send(j, carry):
+                window_copy(rounds - 1, j).start()
+                return carry
+
+            lax.fori_loop(0, half, send, 0)
+
+        @pl.when(g < stages)
+        def _():
+            hail(g)
+
         for i in range(GROUP):
             window_copy(r, j + i).wait_recv()
         seconds = spectra([arrived[r, j + i] for i in range(GROUP)], fore_row_ref[...], fore_col_ref[...])
@@ -436,7 +457,11 @@
         )
         own = r * slots + pick(r, sides) * half + j
         other = r * slots + (1 - pick(r, sides)) * half + j
-        pl.semaphore_wait(hello.at[early + g], 1)
+
+        @pl.when(g < stages)
+        def _():
+            pl.semaphore_wait(hello.at[g], 1)
+
         return (
             disp
             + row_place(a, own)
@@ -445,10 +470,6 @@
             + row_place(d, other + entries)
         )
 
-    early = stages - rounds * parts
-    for i in range(early):
-        hail(i)
-        pl.semaphore_wait(hello.at[i], 1)
     for s in range(rounds):
         line_copy(s).wait()
     ids = line[...]
@@ -458,7 +479,11 @@
         in_round = (lane >= s * slots) & (lane < (s + 1) * slots)
         mine = (lane // half) % 2 == sides[s]
         id_line = id_line + jnp.where(in_round, jnp.where(mine, ids, theirs), 0.0)
-    disp = lax.fori_loop(0, rounds * parts, work, pltpu.roll(id_line, 2 * entries, 1))
+    done = rounds * parts
+    for i in range(done, stages):
+        hail(i)
+        pl.semaphore_wait(hello.at[i], 1)
+    disp = lax.fori_loop(0, done, work, pltpu.roll(id_line, 2 * entries, 1))
 
     tile_out[...] = disp
     tiles[me] = disp
@@ -557,7 +582,7 @@
             pltpu.VMEM((1, LANES), F32),
             pltpu.VMEM((devices, 1, LANES), F32),
             sem((4,)),
-            sem((rounds,)),
+            sem((rounds, CUTS)),
             sem((4,)),
             sem((rounds, half)),
             sem((rounds, half)),

time: 26.2 us -> 25.7 us (0.981)
  Pallas kernels: 25.5 us -> 24.9 us
    pallas_call x1, Pallas kernels: 25.5 us -> 24.9 us  [on_device(): pl.pallas_call(stitch, out_shape=jax.ShapeDtypeStruct((2, NODE_DEV), F32)...]
where the time goes in v6:
time: 25.7 us; the launch traced here: 25.5 us
  Pallas kernels  24.9 us (97%)
  local copies, waits for them, and re-layouts  0.56 us (2%)
    pallas_call x1, Pallas kernels, on_device(): pl.pallas_call(stitch, out_shape=jax.ShapeDtypeStruct((2, NODE_DEV), F32)...  24.9 us
    unnamed x1, local copies, waits for them, and re-layouts  0.56 us

profile of v6, /device:TPU:0, one launch (start us, length us, event | category | flops | bytes accessed | tf_op | source)
XLA Modules:
  0.0 25.5 jit_solution(3190065134969974367)
XLA Ops:
  0.0 24.9 %stitch.1 = f32[2,128]{1,0:T(2,128)S(1)} custom-call(s32[1,2]{1,0:T(1,128)} %colour_hbm.1, s32[1,2,2,16]{3,2,1,0:T(2,128)} %bitcast.5, s32[1,2]{1,0:T(1,128)} %live_hbm.1, s32[1,2,16]{2,1,0:T(2,128)} %ids_hbm.1, bf16[2,32,32,8,128]{4,3,2,1,0:T(8,128)(2,1)} %bitcast.4, bf16[128,256]{1,0:T(8,128)(2,1)} %constant.8.clone.fore_row_hbm, ...), custom_call_target="tpu_custom_call" | custom-call | tf_op jit(solution)/shard_map/stitch/pallas_call | solution.py:563
  24.9 0.6 %copy.11 = f32[2,128]{1,0:T(2,128)} copy(f32[2,128]{1,0:T(2,128)S(1)} %stitch.1) | data formatting | bytes 2048

commit v7 on v6

--- a/solution.py
+++ b/solution.py
@@ -17,8 +17,7 @@
 CUTS = 2
 SUB = 8
 DOT = 2
-LATE = (0,)
-LATE_STEP = 1
+LATE = {0: (1, 0), 3: (1, 4)}
 VMEM_LIMIT = 32 * 1024 * 1024
 
 F32 = jnp.float32
@@ -393,14 +392,19 @@
         for i, window in enumerate(extract(r, [base + i for i in range(PAIR)])):
             sent[r, j + i] = window
 
-        @pl.when((q > 0) & ((place_of(q - 1)[0] < rounds - 1) | jnp.logical_not(late)))
+        before, window = place_of(q - 1)
+
+        @pl.when((q > 0) & ((before < rounds - 1) | (window < late_from)))
         def _():
             launch(q - 1)
 
         return carry
 
     quarter = tile_index // (tile_count // 4)
-    late = functools.reduce(jnp.logical_or, [quarter == v for v in LATE])
+    late_from, late_step = half, -1
+    for at, (step, window) in LATE.items():
+        late_from = jnp.where(quarter == at, window, late_from)
+        late_step = jnp.where(quarter == at, step, late_step)
     lax.fori_loop(0, rounds * half // PAIR, produce, 0)
     for load in table_loads:
         load.wait()
@@ -434,13 +438,13 @@
         r, part = g // parts, g % parts
         j = part * GROUP
 
-        @pl.when(late & (g == LATE_STEP))
+        @pl.when(g == late_step)
         def _():
             def send(j, carry):
                 window_copy(rounds - 1, j).start()
                 return carry
 
-            lax.fori_loop(0, half, send, 0)
+            lax.fori_loop(late_from, half, send, 0)
 
         @pl.when(g < stages)
         def _():

time: 25.7 us -> 25.4 us (0.988)
  no operation moved by 1% of the time
where the time goes in v7:
time: 25.4 us; the launch traced here: 25.2 us
  Pallas kernels  24.7 us (97%)
  local copies, waits for them, and re-layouts  0.56 us (2%)
    pallas_call x1, Pallas kernels, on_device(): pl.pallas_call(stitch, out_shape=jax.ShapeDtypeStruct((2, NODE_DEV), F32)...  24.7 us
    unnamed x1, local copies, waits for them, and re-layouts  0.56 us

profile of v7, /device:TPU:0, one launch (start us, length us, event | category | flops | bytes accessed | tf_op | source)
XLA Modules:
  0.0 25.2 jit_solution(6969834546518186592)
XLA Ops:
  0.0 24.7 %stitch.1 = f32[2,128]{1,0:T(2,128)S(1)} custom-call(s32[1,2]{1,0:T(1,128)} %colour_hbm.1, s32[1,2,2,16]{3,2,1,0:T(2,128)} %bitcast.5, s32[1,2]{1,0:T(1,128)} %live_hbm.1, s32[1,2,16]{2,1,0:T(2,128)} %ids_hbm.1, bf16[2,32,32,8,128]{4,3,2,1,0:T(8,128)(2,1)} %bitcast.4, bf16[128,256]{1,0:T(8,128)(2,1)} %constant.8.clone.fore_row_hbm, ...), custom_call_target="tpu_custom_call" | custom-call | tf_op jit(solution)/shard_map/stitch/pallas_call | solution.py:567
  24.7 0.6 %copy.11 = f32[2,128]{1,0:T(2,128)} copy(f32[2,128]{1,0:T(2,128)S(1)} %stitch.1) | data formatting | bytes 2048

commit v8 on v7

--- a/solution.py
+++ b/solution.py
@@ -17,7 +17,7 @@
 CUTS = 2
 SUB = 8
 DOT = 2
-LATE = {0: (1, 0), 3: (1, 4)}
+LATE = {0: (1, 0), 3: (0, 0)}
 VMEM_LIMIT = 32 * 1024 * 1024
 
 F32 = jnp.float32
@@ -379,7 +379,7 @@
         line_copy(r).start()
 
     def place_of(q):
-        return rounds - 1 - q % rounds, (q // rounds) * PAIR
+        return rounds - 1 - q // (half // PAIR), q % (half // PAIR) * PAIR
 
     def launch(q):
         r, j = place_of(q)

time: 25.4 us -> 25.4 us (level)
  no operation moved by 1% of the time
where the time goes in v8:
time: 25.4 us; the launch traced here: 25.2 us
  Pallas kernels  24.7 us (97%)
  local copies, waits for them, and re-layouts  0.56 us (2%)
    pallas_call x1, Pallas kernels, on_device(): pl.pallas_call(stitch, out_shape=jax.ShapeDtypeStruct((2, NODE_DEV), F32)...  24.7 us
    unnamed x1, local copies, waits for them, and re-layouts  0.56 us

profile of v8, /device:TPU:0, one launch (start us, length us, event | category | flops | bytes accessed | tf_op | source)
XLA Modules:
  0.0 25.2 jit_solution(3750487232936355455)
XLA Ops:
  0.0 24.7 %stitch.1 = f32[2,128]{1,0:T(2,128)S(1)} custom-call(s32[1,2]{1,0:T(1,128)} %colour_hbm.1, s32[1,2,2,16]{3,2,1,0:T(2,128)} %bitcast.5, s32[1,2]{1,0:T(1,128)} %live_hbm.1, s32[1,2,16]{2,1,0:T(2,128)} %ids_hbm.1, bf16[2,32,32,8,128]{4,3,2,1,0:T(8,128)(2,1)} %bitcast.4, bf16[128,256]{1,0:T(8,128)(2,1)} %constant.8.clone.fore_row_hbm, ...), custom_call_target="tpu_custom_call" | custom-call | tf_op jit(solution)/shard_map/stitch/pallas_call | solution.py:567
  24.7 0.6 %copy.11 = f32[2,128]{1,0:T(2,128)} copy(f32[2,128]{1,0:T(2,128)S(1)} %stitch.1) | data formatting | bytes 2048

commit v9 on v8

--- a/solution.py
+++ b/solution.py
@@ -13,7 +13,7 @@
 NODE_DEV = 128
 LANES = 128
 GROUP = 4
-PAIR = 2
+PAIR = 4
 CUTS = 2
 SUB = 8
 DOT = 2

time: 25.4 us -> 25.4 us (level)
  no operation moved by 1% of the time
where the time goes in v9:
time: 25.4 us; the launch traced here: 25.2 us
  Pallas kernels  24.7 us (97%)
  local copies, waits for them, and re-layouts  0.56 us (2%)
    pallas_call x1, Pallas kernels, on_device(): pl.pallas_call(stitch, out_shape=jax.ShapeDtypeStruct((2, NODE_DEV), F32)...  24.7 us
    unnamed x1, local copies, waits for them, and re-layouts  0.56 us

profile of v9, /device:TPU:0, one launch (start us, length us, event | category | flops | bytes accessed | tf_op | source)
XLA Modules:
  0.0 25.2 jit_solution(10099654636689777185)
XLA Ops:
  0.0 24.7 %stitch.1 = f32[2,128]{1,0:T(2,128)S(1)} custom-call(s32[1,2]{1,0:T(1,128)} %colour_hbm.1, s32[1,2,2,16]{3,2,1,0:T(2,128)} %bitcast.5, s32[1,2]{1,0:T(1,128)} %live_hbm.1, s32[1,2,16]{2,1,0:T(2,128)} %ids_hbm.1, bf16[2,32,32,8,128]{4,3,2,1,0:T(8,128)(2,1)} %bitcast.4, bf16[128,256]{1,0:T(8,128)(2,1)} %constant.8.clone.fore_row_hbm, ...), custom_call_target="tpu_custom_call" | custom-call | tf_op jit(solution)/shard_map/stitch/pallas_call | solution.py:567
  24.7 0.6 %copy.11 = f32[2,128]{1,0:T(2,128)} copy(f32[2,128]{1,0:T(2,128)S(1)} %stitch.1) | data formatting | bytes 2048
